TPU v7x, 32 devices: a whole 2x2x4 slice. The times are simulated.
32 devices in a mesh: dom: 16 (over z, y, x), band: 2 (over core).
Axes of the slice: x: 2, y: 2, z: 4, core: 2. Of those that a mesh axis runs over, the one named last changes fastest.
Arguments:
- wavefunctions: bfloat16 [32768, 1024], P('dom', 'band'), may hold values from -4 to 4
- mass_scale: float32 [32768], P('dom'), may hold values from 0.7 to 1.4
- cell_matrices: bfloat16 [128, 512, 512], P('dom')
- connectivity: int32 [128, 512], P('dom'), may hold values from 0 to 2303, as said below
- face_index: int32 [4096], P('dom'), may hold values from 0 to 2047, as said below
Outputs:
- rotated: float32 [32768, 1024], P('dom', 'band')
Inputs may be any that keep to these rules, and one draw needn't show every extreme that they name: `connectivity`: local numbers of each cell's 512 nodes within its domain: below 2048 the domain's own nodes, from 2048 on the entries of the next domain's face list in order; every local number appears in its domain, and a number may repeat. `face_index`: local numbers of 256 own nodes of each domain, in the order that the previous domain uses; a number may repeat.
All inputs are finite; a program needn't handle non-finite values.
Results may differ from a plain program's by a relative error of at most 0.011.
Values may be sent and summed in bfloat16 or wider, within the bound.
A program may use at most 64 MiB of HBM per device.

v0:
```python
import functools

import jax
import jax.numpy as jnp
from jax import lax
from jax.experimental import pallas as pl
from jax.experimental.pallas import tpu as pltpu
from jax.sharding import PartitionSpec as P

filter_center = 5.0
filter_half = 5.0
MESH = pl.DeviceIdType.MESH
VMEM_LIMIT = 62 * 1024 * 1024


def row_tile(rows, most):
    return max(t for t in range(16, most + 1, 16) if rows % t == 0)


def dot32(a, b, dims=((1,), (0,))):
    return lax.dot_general(a, b, (dims, ((), ())), preferred_element_type=jnp.float32)


def operator_kernel(share, conn_ref, a_ref, m_ref, ht, b, send_sem, recv_sem):
    cells, nodes = conn_ref.shape
    extent, width = m_ref.shape[1], b.shape[1]
    me = lax.axis_index("band") if share > 1 else 0
    if share > 1:
        barrier = pltpu.get_barrier_semaphore()
        for step in range(1, share):
            peer = lax.rem(me + step, share)
            pl.semaphore_signal(barrier, inc=1, device_id={"band": peer}, device_id_type=MESH)
        pl.semaphore_wait(barrier, share - 1)
    build = row_tile(extent, 256)

    @pl.loop(0, cells)
    def _(c):
        links = conn_ref[pl.ds(c, 1), :]
        span = pl.ds(pl.multiple_of(c * nodes, 128), nodes)

        @pl.loop(0, extent // build)
        def _(r):
            ids = lax.broadcasted_iota(jnp.int32, (build, nodes), 0) + r * build
            ht[pl.ds(pl.multiple_of(r * build, build), build), span] = jnp.where(
                ids == links, 1.0, 0.0
            ).astype(jnp.bfloat16)

    first = pl.multiple_of(me * width, 128) if share > 1 else 0

    @pl.loop(0, cells)
    def _(c):
        span = pl.ds(pl.multiple_of(c * nodes, 128), nodes)
        picks = ht[pl.ds(first, width), span]
        b[span, :] = dot32(a_ref[c], picks, ((1,), (1,))).astype(jnp.bfloat16)

    tile = row_tile(extent, 384)
    tiles = extent // tile

    def copies(r):
        rows = pl.ds(pl.multiple_of(r * tile, tile), tile)
        return [
            pltpu.make_async_remote_copy(
                src_ref=m_ref.at[me, rows],
                dst_ref=m_ref.at[me, rows],
                send_sem=send_sem.at[step, r],
                recv_sem=recv_sem.at[step, r],
                device_id={"band": lax.rem(me + step, share)},
                device_id_type=MESH,
            )
            for step in range(1, share)
        ]

    @pl.loop(0, tiles)
    def _(r):
        rows = pl.ds(pl.multiple_of(r * tile, tile), tile)
        total = dot32(ht[rows, :], b[...])
        kept = total.astype(jnp.bfloat16)
        m_ref[me, rows, :width] = kept
        offsets = lax.broadcasted_iota(jnp.int32, (tile, width), 1) - lax.broadcasted_iota(
            jnp.int32, (tile, width), 0
        )
        rest = jnp.where(
            offsets == r * tile - me * width, total - kept.astype(jnp.float32), 0.0
        )
        rest = jnp.sum(rest, axis=1, keepdims=True)
        m_ref[me, rows, width:] = jnp.broadcast_to(rest, (tile, 128)).astype(jnp.bfloat16)
        for copy in copies(r):
            copy.start()

    @pl.loop(0, tiles)
    def _(r):
        for copy in copies(r):
            copy.wait()


def domain_operator(cell_matrices, connectivity, extent):
    cells, nodes = connectivity.shape
    share = lax.axis_size("band")
    if extent % (share * 128):
        share = 1
    width = extent // share
    tiles = extent // row_tile(extent, 384)
    vmem = pl.BlockSpec(memory_space=pltpu.VMEM)
    params = dict(collective_id=0, has_side_effects=True) if share > 1 else {}
    halves = pl.pallas_call(
        functools.partial(operator_kernel, share),
        out_shape=jax.ShapeDtypeStruct((share, extent, width + 128), jnp.bfloat16),
        in_specs=[vmem] * 2,
        out_specs=vmem,
        scratch_shapes=[
            pltpu.VMEM((extent, cells * nodes), jnp.bfloat16),
            pltpu.VMEM((cells * nodes, width), jnp.bfloat16),
            pltpu.SemaphoreType.DMA((share, tiles)),
            pltpu.SemaphoreType.DMA((share, tiles)),
        ],
        compiler_params=pltpu.CompilerParams(vmem_limit_bytes=VMEM_LIMIT, **params),
        name="domain_operator",
    )(connectivity, cell_matrices)
    rest = sum(halves[i, :, width:].astype(jnp.float32) for i in range(share))
    return jnp.concatenate([halves[i, :, :width] for i in range(share)], axis=1), rest


def passed_along(value, axis, steps):
    count = lax.axis_size(axis)
    initial, last = (max(0, -steps), min(count, count - steps))
    return lax.ppermute(value, axis, [(source, source + steps) for source in range(initial, last)])


def on_device(wavefunctions, mass_scale, cell_matrices, connectivity, face_index):
    bf16 = jnp.bfloat16
    own, band_width = wavefunctions.shape
    face = face_index.shape[0]
    domains = lax.axis_size("dom")
    states = band_width * lax.axis_size("band")
    matrix, rest = domain_operator(cell_matrices, connectivity, own + face)
    face_of = (face_index[:, None] == lax.broadcasted_iota(jnp.int32, (face, own), 1)).astype(bf16)
    face_in = (face_index[None, :] == lax.broadcasted_iota(jnp.int32, (own, face), 0)).astype(bf16)
    outgoing = jnp.concatenate([matrix[own:, :own], face_of], axis=0)
    inner = matrix[:own, :own]
    edge = jnp.concatenate([matrix[:own, own:], face_in, face_in], axis=1)
    corner = jnp.concatenate([matrix[own:, own:], rest[own:].astype(bf16)], axis=1)
    corner = passed_along(corner, "dom", 1)
    corner, corner_rest = corner[:, :face], corner[:, face : face + 1].astype(jnp.float32)
    rest = rest[:own, :1]
    mass = mass_scale[:, None]

    def hamiltonian(vectors):
        scaled = (mass * vectors).astype(bf16)
        sent = dot32(outgoing, scaled).astype(bf16)
        returned = passed_along(sent[:face], "dom", 1)
        received = passed_along(sent[face:], "dom", -1)
        summed = dot32(inner, scaled) + rest * scaled.astype(jnp.float32)
        added = returned.astype(jnp.float32) + dot32(corner, sent[face:])
        added = added + corner_rest * sent[face:].astype(jnp.float32)
        high = added.astype(bf16)
        low = (added - lax.reduce_precision(added, 8, 7)).astype(bf16)
        summed = summed + dot32(edge, jnp.concatenate([received, high, low], axis=0))
        return mass * summed

    previous = wavefunctions.astype(jnp.float32)
    current = (hamiltonian(previous) - filter_center * previous) / filter_half
    for _ in range(2):
        following = 2.0 * (hamiltonian(current) - filter_center * current) / filter_half - previous
        previous, current = (current, following)
    rounded = current.astype(bf16)
    everyone = lax.all_gather(rounded, "band", axis=1, tiled=True)
    partial = dot32(everyone, rounded, ((0,), (0,))) / (own * domains)
    tile = lax.psum_scatter(partial.astype(bf16), "dom", scatter_dimension=0, tiled=True)
    columns = lax.all_gather(tile, "dom", axis=0, tiled=True)
    margin = lax.all_gather(columns, "band", axis=1, tiled=True).astype(jnp.float32)
    identity = (
        lax.broadcasted_iota(jnp.int32, (states, states), 0)
        == lax.broadcasted_iota(jnp.int32, (states, states), 1)
    ).astype(jnp.float32)
    mean_eigen = jnp.sum(margin * identity) / states
    offset = (margin / mean_eigen - identity).astype(bf16)
    start = lax.axis_index("band") * band_width
    first = lax.dynamic_slice_in_dim(columns.astype(jnp.float32), 0, states, 0) / mean_eigen
    first = first - lax.dynamic_slice_in_dim(identity, start, band_width, 1)
    second = dot32(offset, first.astype(bf16))
    third = dot32(offset, second.astype(bf16))
    tail = dot32(offset, (third / 16.0 - second * (5.0 / 16.0)).astype(bf16))
    change = tail + 0.375 * second - 0.5 * first
    turned = current + dot32(everyone, change.astype(bf16))
    return turned / jnp.sqrt(mean_eigen)


def solution(mesh):
    return jax.shard_map(
        on_device,
        mesh=mesh,
        in_specs=(P("dom", "band"), P("dom"), P("dom", None, None), P("dom", None), P("dom")),
        out_specs=P("dom", "band"),
        check_vma=False,
    )
```

profile of v0, /device:TPU:0, one launch (start us, length us, event | category | flops | bytes accessed | tf_op | source)
XLA Modules:
  0.0 332.4 jit_solution(7075075881628874042)
XLA Ops:
  6.5 47.1 %domain_operator.1 = bf16[2,2304,1280]{2,1,0:T(8,128)(2,1)} custom-call(s32[8,512]{1,0:T(8,128)} %conn_ref.1, bf16[8,512,512]{2,1,0:T(8,128)(2,1)} %a_ref.1), custom_call_target="tpu_custom_call" | custom-call | tf_op jit(solution)/shard_map/domain_operator/pallas_call | solution.py:105
  53.7 1.4 convert_add_fusion
  55.1 8.8 %slice_bitcast_fusion = (bf16[2304,1152]{1,0:T(8,128)(2,1)}, bf16[2304,1152]{1,0:T(8,128)(2,1)}) fusion(bf16[2,2304,1280]{2,1,0:T(8,128)(2,1)} %domain_operator.1), kind=kLoop, calls=%fused_computation.6 | loop fusion | bytes 21233664 | tf_op jit(solution)/shard_map/squeeze | solution.py:120
  64.9 4.8 %collective-permute-start.2 = (bf16[256,384]{1,0:T(8,128)(2,1)S(1)}, bf16[256,384]{1,0:T(8,128)(2,1)S(1)}, u32[]{:S(2)}, u32[]{:S(2)}) collective-permute-start(bf16[256,384]{1,0:T(8,128)(2,1)S(1)} %pad_maximum_fusion.5), channel_id=1, source_target_pairs={{0,2},{2,4},{4,6},{6,8},{8,10},{10,12},{12,14},{14,16},{16,18},{18... | collective-permute-start | bytes 589832 | tf_op jit(solution)/shard_map/ppermute | solution.py:126
  70.0 1.6 fusion.7
  72.0 1.4 convolution_convert_fusion.2
  73.4 1.4 collective-permute-start
  74.9 5.1 %collective-permute-start.1 = (bf16[256,512]{1,0:T(8,128)(2,1)S(1)}, bf16[256,512]{1,0:T(8,128)(2,1)S(1)}, u32[]{:S(2)}, u32[]{:S(2)}) collective-permute-start(bf16[256,512]{1,0:T(8,128)(2,1)S(1)} %get-tuple-element.16), channel_id=1, source_target_pairs={{0,2},{2,4},{4,6},{6,8},{8,10},{10,12},{12,14},{14,16},{16,18},{18... | collective-permute-start | bytes 786440 | tf_op jit(solution)/shard_map/ppermute | solution.py:126
  80.5 1.4 fusion.58
  83.1 4.8 %fusion.31 = f32[2048,512]{1,0:T(8,128)S(1)} fusion(bf16[2048,2048]{1,0:T(8,128)(2,1)S(1)} %fusion, bf16[2048,512]{1,0:T(8,128)(2,1)S(1)} %copy-done.4, f32[2048]{0:T(1024)S(1)} %copy-done.2), kind=kOutput, calls=%fused_computation.58 | convolution fusion | flops 4298113024 | bytes 14688256 | tf_op jit(solution)/shard_map/dot_general | solution.py:21
  88.4 1.6 collective-permute-done.1
  90.3 2.6 fusion.5
  92.9 1.3 convolution_convert_fusion.1
  95.6 5.2 %collective-permute-start.4 = (bf16[256,512]{1,0:T(8,128)(2,1)S(1)}, bf16[256,512]{1,0:T(8,128)(2,1)S(1)}, u32[]{:S(2)}, u32[]{:S(2)}) collective-permute-start(bf16[256,512]{1,0:T(8,128)(2,1)S(1)} %get-tuple-element.12), channel_id=1, source_target_pairs={{0,2},{2,4},{4,6},{6,8},{8,10},{10,12},{12,14},{14,16},{16,18},{18... | collective-permute-start | bytes 786440 | tf_op jit(solution)/shard_map/ppermute | solution.py:126
  100.7 4.8 %fusion.60 = f32[2048,512]{1,0:T(8,128)S(1)} fusion(bf16[2048,2048]{1,0:T(8,128)(2,1)S(1)} %fusion, f32[2048,512]{1,0:T(8,128)S(1)} %fusion.5, f32[2048]{0:T(1024)S(1)} %broadcast_multiply_fusion), kind=kOutput, calls=%fused_computation.87 | convolution fusion | flops 4297064448 | bytes 16785408 | tf_op jit(solution)/shard_map/dot_general | solution.py:21
  105.5 4.8 %collective-permute-done.4 = bf16[256,512]{1,0:T(8,128)(2,1)S(1)} collective-permute-done((bf16[256,512]{1,0:T(8,128)(2,1)S(1)}, bf16[256,512]{1,0:T(8,128)(2,1)S(1)}, u32[]{:S(2)}, u32[]{:S(2)}) %collective-permute-start.4) | collective-permute-done | bytes 262176 | tf_op jit(solution)/shard_map/ppermute | solution.py:126
  110.6 3.1 convert_subtract_fusion
  113.7 1.4 convolution_convert_fusion
  116.5 5.2 %collective-permute-start.6 = (bf16[256,512]{1,0:T(8,128)(2,1)S(1)}, bf16[256,512]{1,0:T(8,128)(2,1)S(1)}, u32[]{:S(2)}, u32[]{:S(2)}) collective-permute-start(bf16[256,512]{1,0:T(8,128)(2,1)S(1)} %get-tuple-element.8), channel_id=1, source_target_pairs={{0,2},{2,4},{4,6},{6,8},{8,10},{10,12},{12,14},{14,16},{16,18},{18... | collective-permute-start | bytes 786440 | tf_op jit(solution)/shard_map/ppermute | solution.py:126
  121.7 4.8 %fusion.59 = f32[2048,512]{1,0:T(8,128)S(1)} fusion(bf16[2048,2048]{1,0:T(8,128)(2,1)S(1)} %fusion, f32[2048,512]{1,0:T(8,128)S(1)} %convert_subtract_fusion, f32[2048]{0:T(1024)S(1)} %copy-done.2), kind=kOutput, calls=%fused_computation.86 | convolution fusion | flops 4297064448 | bytes 16785408 | tf_op jit(solution)/shard_map/dot_general | solution.py:21
  126.5 5.0 %collective-permute-done.6 = bf16[256,512]{1,0:T(8,128)(2,1)S(1)} collective-permute-done((bf16[256,512]{1,0:T(8,128)(2,1)S(1)}, bf16[256,512]{1,0:T(8,128)(2,1)S(1)}, u32[]{:S(2)}, u32[]{:S(2)}) %collective-permute-start.6) | collective-permute-done | bytes 262176 | tf_op jit(solution)/shard_map/ppermute | solution.py:126
  131.8 4.7 %fusion.70 = (bf16[2048,512]{1,0:T(8,128)(2,1)}, f32[2048,512]{1,0:T(8,128)}) fusion(f32[2048,512]{1,0:T(8,128)S(1)} %fusion.5, f32[2048,512]{1,0:T(8,128)S(1)} %convert_subtract_fusion, bf16[256,512]{1,0:T(8,128)(2,1)S(1)} %get-tuple-element.10, bf16[256,512]{1,0:T(8,128)(2,1)S(1)} %get-tuple-element.9, bf16[256,512]{1,0:T(8,128)(2,1)S(1)} %collective-permute-done.5, ...), kind=kOutput, calls=%fused_computation.94 | convolution fusion | flops 1636040704 | bytes 21774336 | tf_op jit(solution)/shard_map/dot_general | solution.py:21
  136.6 14.4 %all-gather.4.cloned.1.call-done = bf16[2048,1024]{1,0:T(8,128)(2,1)} async-done(((bf16[2048,512]{1,0:T(8,128)(2,1)}), bf16[2048,1024]{1,0:T(8,128)(2,1)}) %all-gather.4.cloned.1.call-update) | async-done | bytes 4194320 | tf_op jit(solution)/shard_map/all_gather | solution.py:166
  150.9 6.2 %multiply_convert_fusion.2 = bf16[1024,512]{1,0:T(8,128)(2,1)} fusion(bf16[2048,1024]{1,0:T(8,128)(2,1)} %all-gather.4.cloned.1.call-done, bf16[2048,512]{1,0:T(8,128)(2,1)} %get-tuple-element.19), kind=kOutput, calls=%fused_computation.27 | convolution fusion | flops 2148532224 | bytes 7340032 | tf_op jit(solution)/shard_map/dot_general | solution.py:21
  157.2 80.0 %reduce-scatter.2.cloned.1.call-done = bf16[64,512]{1,0:T(8,128)(2,1)} async-done(((bf16[1024,512]{1,0:T(8,128)(2,1)}), bf16[64,512]{1,0:T(8,128)(2,1)}) %reduce-scatter.2.cloned.1.call-update) | async-done | bytes 65552 | tf_op jit(solution)/shard_map/reduce_scatter | solution.py:168
  237.5 53.9 %all-gather.6.cloned.1.call-done = bf16[1024,512]{1,0:T(8,128)(2,1)} async-done(((bf16[64,512]{1,0:T(8,128)(2,1)}), bf16[1024,512]{1,0:T(8,128)(2,1)}) %all-gather.6.cloned.1.call-update) | async-done | bytes 1048592 | tf_op jit(solution)/shard_map/all_gather | solution.py:169
  291.5 2.5 fusion.6
  294.0 8.3 %all-gather.8.cloned.1.call-done = bf16[1024,1024]{1,0:T(8,128)(2,1)} async-done(((bf16[1024,512]{1,0:T(8,128)(2,1)}), bf16[1024,1024]{1,0:T(8,128)(2,1)}) %all-gather.8.cloned.1.call-update) | async-done | bytes 2097168 | tf_op jit(solution)/shard_map/all_gather | solution.py:170
  302.3 2.4 fusion.1
  305.3 5.0 %fusion.11 = f32[1024,512]{1,0:T(8,128)} fusion(f32[1024,1024]{1,0:T(8,128)} %fusion.6, s32[]{:T(128)S(6)} %select_n.3, bf16[1024,512]{1,0:T(8,128)(2,1)S(1)} %copy-done.1, f32[]{:T(128)S(6)} %div.50, bf16[1024,1024]{1,0:T(8,128)(2,1)} %all-gather.8.cloned.1.call-done), kind=kOutput, calls=%fused_computation.38 | convolution fusion | flops 1082130432 | bytes 7341568 | tf_op jit(solution)/shard_map/dot_general | solution.py:21
  310.4 7.1 %subtract_convert_fusion = bf16[1024,512]{1,0:T(8,128)(2,1)} fusion(f32[1024,512]{1,0:T(8,128)} %fusion.11, f32[1024,1024]{1,0:T(8,128)} %fusion.6, s32[]{:T(128)S(6)} %select_n.3, f32[]{:T(128)S(6)} %div.50, bf16[1024,512]{1,0:T(8,128)(2,1)S(1)} %copy-done.1, bf16[1024,1024]{1,0:T(8,128)(2,1)S(1)} %copy-done), kind=kOutput, calls=%fused_computation.24 | convolution fusion | flops 2166882304 | bytes 14682112 | tf_op jit(solution)/shard_map/dot_general | solution.py:21
  317.5 8.1 %add_divide_fusion = f32[2048,512]{1,0:T(8,128)} fusion(f32[2048,512]{1,0:T(8,128)} %get-tuple-element.20, bf16[2048,1024]{1,0:T(8,128)(2,1)} %all-gather.4.cloned.1.call-done, bf16[1024,512]{1,0:T(8,128)(2,1)} %subtract_convert_fusion, f32[]{:T(128)S(6)} %sqrt.3), kind=kOutput, calls=%fused_computation.15 | convolution fusion | flops 2149580800 | bytes 13631492 | tf_op jit(solution)/shard_map/dot_general | solution.py:21
  (50 shorter events, 7.8 us)
Async XLA Ops:
  6.5 144.4 %all-gather.4.cloned.1.call-start = ((), (), s32[]{:S(2)}) async-start(), calls=%async_computation.1 | async-start | bytes 6291456 | tf_op jit(solution)/shard_map/all_gather | solution.py:166
  55.1 14.6 %copy-start.3 = (s32[256]{0:T(256)S(1)}, s32[256]{0:T(256)}, u32[]{:S(2)}) copy-start(s32[256]{0:T(256)} %param.9) | copy-start | bytes 3076
  64.9 23.4 %collective-permute-start.2 = (bf16[256,384]{1,0:T(8,128)(2,1)S(1)}, bf16[256,384]{1,0:T(8,128)(2,1)S(1)}, u32[]{:S(2)}, u32[]{:S(2)}) collective-permute-start(bf16[256,384]{1,0:T(8,128)(2,1)S(1)} %pad_maximum_fusion.5), channel_id=1, source_target_pairs={{0,2},{2,4},{4,6},{6,8},{8,10},{10,12},{12,14},{14,16},{16,18},{18... | collective-permute-start | bytes 589832 | tf_op jit(solution)/shard_map/ppermute | solution.py:126
  69.9 11.9 %slice-start = ((s8[5308416]{0:T(1024)(128)(4,1)}), s8[4194304]{0:T(1024)(128)(4,1)S(1)}, s32[]{:S(2)}) async-start(s8[5308416]{0:T(1024)(128)(4,1)} %bitcast.18), calls=%async_computation.5 | async-start | bytes 8388608
  69.9 11.9 %slice-start.2 = ((s8[5308416]{0:T(1024)(128)(4,1)}), s8[4194304]{0:T(1024)(128)(4,1)S(1)}, s32[]{:S(2)}) async-start(s8[5308416]{0:T(1024)(128)(4,1)} %bitcast.20), calls=%async_computation.7 | async-start | bytes 8388608
  70.0 1.6 copy-start.2
  70.0 2.1 copy-start.4
  70.0 11.9 %slice-start.1 = ((s8[5308416]{0:T(1024)(128)(4,1)}), s8[1114112]{0:T(1024)(128)(4,1)S(1)}, s32[]{:S(2)}) async-start(s8[5308416]{0:T(1024)(128)(4,1)} %bitcast.18), calls=%async_computation.6 | async-start | bytes 2228224
  70.0 11.9 %slice-start.3 = ((s8[5308416]{0:T(1024)(128)(4,1)}), s8[1114112]{0:T(1024)(128)(4,1)S(1)}, s32[]{:S(2)}) async-start(s8[5308416]{0:T(1024)(128)(4,1)} %bitcast.20), calls=%async_computation.8 | async-start | bytes 2228224
  73.4 16.9 %collective-permute-start = (bf16[256,512]{1,0:T(8,128)(2,1)S(1)}, bf16[256,512]{1,0:T(8,128)(2,1)S(1)}, u32[]{:S(2)}, u32[]{:S(2)}) collective-permute-start(bf16[256,512]{1,0:T(8,128)(2,1)S(1)} %get-tuple-element.15), channel_id=1, source_target_pairs={{2,0},{4,2},{6,4},{8,6},{10,8},{12,10},{14,12},{16,14},{18,16},{20... | collective-permute-start | bytes 786440 | tf_op jit(solution)/shard_map/ppermute | solution.py:126
  74.9 15.1 %collective-permute-start.1 = (bf16[256,512]{1,0:T(8,128)(2,1)S(1)}, bf16[256,512]{1,0:T(8,128)(2,1)S(1)}, u32[]{:S(2)}, u32[]{:S(2)}) collective-permute-start(bf16[256,512]{1,0:T(8,128)(2,1)S(1)} %get-tuple-element.16), channel_id=1, source_target_pairs={{0,2},{2,4},{4,6},{6,8},{8,10},{10,12},{12,14},{14,16},{16,18},{18... | collective-permute-start | bytes 786440 | tf_op jit(solution)/shard_map/ppermute | solution.py:126
  94.3 16.4 %collective-permute-start.3 = (bf16[256,512]{1,0:T(8,128)(2,1)S(1)}, bf16[256,512]{1,0:T(8,128)(2,1)S(1)}, u32[]{:S(2)}, u32[]{:S(2)}) collective-permute-start(bf16[256,512]{1,0:T(8,128)(2,1)S(1)} %get-tuple-element.11), channel_id=1, source_target_pairs={{2,0},{4,2},{6,4},{8,6},{10,8},{12,10},{14,12},{16,14},{18,16},{20... | collective-permute-start | bytes 786440 | tf_op jit(solution)/shard_map/ppermute | solution.py:126
  95.6 14.8 %collective-permute-start.4 = (bf16[256,512]{1,0:T(8,128)(2,1)S(1)}, bf16[256,512]{1,0:T(8,128)(2,1)S(1)}, u32[]{:S(2)}, u32[]{:S(2)}) collective-permute-start(bf16[256,512]{1,0:T(8,128)(2,1)S(1)} %get-tuple-element.12), channel_id=1, source_target_pairs={{0,2},{2,4},{4,6},{6,8},{8,10},{10,12},{12,14},{14,16},{16,18},{18... | collective-permute-start | bytes 786440 | tf_op jit(solution)/shard_map/ppermute | solution.py:126
  115.2 16.6 %collective-permute-start.5 = (bf16[256,512]{1,0:T(8,128)(2,1)S(1)}, bf16[256,512]{1,0:T(8,128)(2,1)S(1)}, u32[]{:S(2)}, u32[]{:S(2)}) collective-permute-start(bf16[256,512]{1,0:T(8,128)(2,1)S(1)} %get-tuple-element.7), channel_id=1, source_target_pairs={{2,0},{4,2},{6,4},{8,6},{10,8},{12,10},{14,12},{16,14},{18,16},{20... | collective-permute-start | bytes 786440 | tf_op jit(solution)/shard_map/ppermute | solution.py:126
  116.5 15.0 %collective-permute-start.6 = (bf16[256,512]{1,0:T(8,128)(2,1)S(1)}, bf16[256,512]{1,0:T(8,128)(2,1)S(1)}, u32[]{:S(2)}, u32[]{:S(2)}) collective-permute-start(bf16[256,512]{1,0:T(8,128)(2,1)S(1)} %get-tuple-element.8), channel_id=1, source_target_pairs={{0,2},{2,4},{4,6},{6,8},{8,10},{10,12},{12,14},{14,16},{16,18},{18... | collective-permute-start | bytes 786440 | tf_op jit(solution)/shard_map/ppermute | solution.py:126
  136.5 100.7 %reduce-scatter.2.cloned.1.call-start = ((), (), s32[]{:S(2)}) async-start(), calls=%async_computation.2 | async-start | bytes 1114112 | tf_op jit(solution)/shard_map/reduce_scatter | solution.py:168
  157.1 134.3 %all-gather.6.cloned.1.call-start = ((), (), s32[]{:S(2)}) async-start(), calls=%async_computation.3 | async-start | bytes 1114112 | tf_op jit(solution)/shard_map/all_gather | solution.py:169
  237.2 65.0 %all-gather.8.cloned.1.call-start = ((), (), s32[]{:S(2)}) async-start(), calls=%async_computation.4 | async-start | bytes 3145728 | tf_op jit(solution)/shard_map/all_gather | solution.py:170
  291.4 13.9 %copy-start.1 = (bf16[1024,512]{1,0:T(8,128)(2,1)S(1)}, bf16[1024,512]{1,0:T(8,128)(2,1)}, u32[]{:S(2)}) copy-start(bf16[1024,512]{1,0:T(8,128)(2,1)} %all-gather.6.cloned.1.call-done) | copy-start | bytes 3145732
  305.3 5.0 %copy-start = (bf16[1024,1024]{1,0:T(8,128)(2,1)S(1)}, bf16[1024,1024]{1,0:T(8,128)(2,1)}, u32[]{:S(2)}) copy-start(bf16[1024,1024]{1,0:T(8,128)(2,1)} %all-gather.8.cloned.1.call-done) | copy-start | bytes 6291460
Sparse Core Ops, SparseCore 0:
  136.6 14.2 all-gather.3
  157.2 79.9 reduce-scatter.1
  240.0 51.3 all-gather.5
  292.8 9.3 all-gather.7
where the time goes:
time: 338 us; the launch traced here: 332 us
  waiting for transfers between devices  168 us (50%)
  matrix products  56.1 us (17%)
  Pallas kernels  47.1 us (14%)
  starting transfers between devices  24.7 us (7%)
  between operations  14.5 us (4%)
  other arithmetic  11.3 us (3%)
  local copies, waits for them, and re-layouts  10.8 us (3%)
    reduce_scatter x1, waiting for transfers between devices, on_device(): lax.psum_scatter(partial.astype(bf16), 'dom', scatter_dimension=0, tiled=...  80 us
    dot_general x16, matrix products, dot32(): lax.dot_general(a, b, (dims, ((), ())), preferred_element_type=jnp.float32)  56.1 us
    all_gather x1, waiting for transfers between devices, on_device(): columns = lax.all_gather(tile, 'dom', axis=0, tiled=True)  53.9 us
    pallas_call x1, Pallas kernels, domain_operator(): pl.pallas_call(functools.partial(operator_kernel, share), out_shape=jax.S...  47.1 us
    ppermute x7, starting transfers between devices, passed_along(): lax.ppermute(value, axis, [(source, source + steps) for source in range(i...  24.3 us
    all_gather x1, waiting for transfers between devices, on_device(): everyone = lax.all_gather(rounded, 'band', axis=1, tiled=True)  14.4 us
    ppermute x7, waiting for transfers between devices, passed_along(): lax.ppermute(value, axis, [(source, source + steps) for source in range(i...  11.4 us
    squeeze x1, local copies, waits for them, and re-layouts, domain_operator(): halves[i, :, :width]  8.85 us
  transfers between devices with their start and end apart: 11, of which 7 were waited for; matrix products, arithmetic and copies ran while one was open for 7% of the time, Pallas kernels for 0%

commit v1 on v0

--- a/solution.py
+++ b/solution.py
@@ -120,6 +120,231 @@
     return jnp.concatenate([halves[i, :, :width] for i in range(share)], axis=1), rest
 
 
+def upper_blocks(band):
+    other = 1 - band
+    return (
+        (2 * band, 2 * band),
+        (2 * band, 2 * band + 1),
+        (2 * band + 1, 2 * band + 1),
+        (2 * band, 2 * other + band),
+        (2 * band + 1, 2 * other + 1 - band),
+    )
+
+
+def split_domains(domains):
+    inner = max(n for n in range(1, domains + 1) if domains % n == 0 and n * n <= domains)
+    return inner, domains // inner
+
+
+def margin_kernel(
+    inner, outer, rounded_ref, everyone_ref, change_ref, scale_ref,
+    part, first_in, first_sum, second_in, gathered, offset, second, third, term,
+    band_send, band_recv, send_one, recv_one, send_two, recv_two,
+    send_three, recv_three, send_four, recv_four, send_five, recv_five,
+):
+    rows, width = rounded_ref.shape
+    states = 2 * width
+    block = width // 2
+    slab = block // inner
+    piece = slab // outer
+    chunks = 5
+    me = lax.axis_index("band")
+    dom = lax.axis_index("dom")
+    high, low = dom // inner, lax.rem(dom, inner)
+    partner = 1 - me
+    plane = [high * inner + lax.rem(low + step, inner) for step in range(1, inner)]
+    line = [lax.rem(high + step, outer) * inner + low for step in range(1, outer)]
+
+    barrier = pltpu.get_barrier_semaphore()
+    for peer in plane + line:
+        pl.semaphore_signal(barrier, inc=1, device_id={"dom": peer}, device_id_type=MESH)
+    pl.semaphore_signal(barrier, inc=1, device_id={"band": partner}, device_id_type=MESH)
+    pl.semaphore_wait(barrier, inner + outer - 1)
+
+    def remote(source, target, sends, recvs, **where):
+        return pltpu.make_async_remote_copy(
+            src_ref=source, dst_ref=target, send_sem=sends, recv_sem=recvs,
+            device_id=where, device_id_type=MESH,
+        )
+
+    mine = pl.ds(pl.multiple_of(me * width, 128), width)
+    across = remote(rounded_ref, everyone_ref.at[:, mine], band_send, band_recv, band=partner)
+    across.start()
+    everyone_ref[:, mine] = rounded_ref[...]
+
+    def plane_copies(c):
+        return [
+            remote(
+                part.at[c, pl.ds(pl.multiple_of(lax.rem(low + step, inner) * slab, slab), slab)],
+                first_in.at[c, step - 1],
+                send_one.at[c, step - 1], recv_one.at[c, step - 1], dom=plane[step - 1],
+            )
+            for step in range(1, inner)
+        ]
+
+    def line_copies(c):
+        return [
+            remote(
+                first_sum.at[c, pl.ds(pl.multiple_of(lax.rem(high + step, outer) * piece, piece), piece)],
+                second_in.at[c, step - 1],
+                send_two.at[c, step - 1], recv_two.at[c, step - 1], dom=line[step - 1],
+            )
+            for step in range(1, outer)
+        ]
+
+    own_slab = pl.ds(pl.multiple_of(low * slab, slab), slab)
+    own_piece = pl.ds(pl.multiple_of(low * slab + high * piece, piece), piece)
+
+    def line_back(c):
+        spot = gathered.at[me, c, own_piece]
+        return [
+            remote(spot, spot, send_three.at[c, s - 1], recv_three.at[c, s - 1], dom=line[s - 1])
+            for s in range(1, outer)
+        ]
+
+    def plane_back(c):
+        spot = gathered.at[me, c, own_slab]
+        return [
+            remote(spot, spot, send_four.at[c, s - 1], recv_four.at[c, s - 1], dom=plane[s - 1])
+            for s in range(1, inner)
+        ]
+
+    def band_back(c):
+        spot = gathered.at[me, c]
+        return remote(spot, spot, send_five.at[c], recv_five.at[c], band=partner)
+
+    share = 1.0 / (rows * inner * outer)
+
+    def emit(c, left, right):
+        part[c] = (dot32(left, right, ((0,), (0,))) * share).astype(jnp.bfloat16)
+        for copy in plane_copies(c):
+            copy.start()
+
+    emit(0, rounded_ref[:, :block], rounded_ref[:, :block])
+    emit(1, rounded_ref[:, :block], rounded_ref[:, block:])
+    emit(2, rounded_ref[:, block:], rounded_ref[:, block:])
+    across.wait()
+    for i in range(2):
+        column = partner * width + (i + me - 2 * i * me) * block
+        emit(
+            3 + i,
+            rounded_ref[:, i * block : (i + 1) * block],
+            everyone_ref[:, pl.ds(pl.multiple_of(column, 128), block)],
+        )
+    for c in range(chunks):
+        total = part[c, own_slab].astype(jnp.float32)
+        for step, copy in enumerate(plane_copies(c)):
+            copy.wait()
+            total = total + first_in[c, step].astype(jnp.float32)
+        first_sum[c] = total.astype(jnp.bfloat16)
+        for copy in line_copies(c):
+            copy.start()
+    for c in range(chunks):
+        total = first_sum[c, pl.ds(pl.multiple_of(high * piece, piece), piece)].astype(jnp.float32)
+        for step, copy in enumerate(line_copies(c)):
+            copy.wait()
+            total = total + second_in[c, step].astype(jnp.float32)
+        gathered[me, c, own_piece] = total.astype(jnp.bfloat16)
+        for copy in line_back(c):
+            copy.start()
+    for c in range(chunks):
+        for copy in line_back(c):
+            copy.wait()
+        for copy in plane_back(c):
+            copy.start()
+    for c in range(chunks):
+        for copy in plane_back(c):
+            copy.wait()
+        band_back(c).start()
+    for c in range(chunks):
+        band_back(c).wait()
+
+    unit = (
+        lax.broadcasted_iota(jnp.int32, (block, block), 0)
+        == lax.broadcasted_iota(jnp.int32, (block, block), 1)
+    ).astype(jnp.float32)
+    trace = 0.0
+    for q in range(2):
+        for c in (0, 2):
+            trace = trace + jnp.sum(gathered[q, c].astype(jnp.float32) * unit)
+    mean_eigen = jnp.full((1, 1), trace, jnp.float32) / states
+    inverse = 1.0 / mean_eigen
+    scale_ref[...] = jnp.broadcast_to(lax.rsqrt(mean_eigen), scale_ref.shape)
+    for q in range(2):
+        for c, (i, j) in enumerate(upper_blocks(q)):
+            value = gathered[q, c].astype(jnp.float32) * inverse
+            if i == j:
+                value = value - unit
+            offset[i * block : (i + 1) * block, j * block : (j + 1) * block] = value.astype(jnp.bfloat16)
+            if i != j:
+                offset[j * block : (j + 1) * block, i * block : (i + 1) * block] = value.T.astype(jnp.bfloat16)
+
+    tiles = states // block
+
+    def span(r):
+        return pl.ds(pl.multiple_of(r * block, block), block)
+
+    @pl.loop(0, tiles)
+    def _(r):
+        value = dot32(offset[span(r), :], offset[:, mine])
+        second[span(r), :] = value
+        term[span(r), :] = value.astype(jnp.bfloat16)
+
+    @pl.loop(0, tiles)
+    def _(r):
+        third[span(r), :] = (
+            dot32(offset[span(r), :], term[...]) / 16.0 - second[span(r), :] * (5.0 / 16.0)
+        ).astype(jnp.bfloat16)
+
+    @pl.loop(0, tiles)
+    def _(r):
+        tail = dot32(offset[span(r), :], third[...])
+        first = offset[span(r), mine].astype(jnp.float32)
+        change_ref[span(r), :] = (tail + 0.375 * second[span(r), :] - 0.5 * first).astype(jnp.bfloat16)
+
+
+def margin_root(rounded, domains):
+    bf16 = jnp.bfloat16
+    rows, width = rounded.shape
+    states, block = 2 * width, width // 2
+    inner, outer = split_domains(domains)
+    slab = block // inner
+    piece = slab // outer
+    vmem = pl.BlockSpec(memory_space=pltpu.VMEM)
+    dma = pltpu.SemaphoreType.DMA
+    return pl.pallas_call(
+        functools.partial(margin_kernel, inner, outer),
+        out_shape=(
+            jax.ShapeDtypeStruct((rows, states), bf16),
+            jax.ShapeDtypeStruct((states, width), bf16),
+            jax.ShapeDtypeStruct((8, 128), jnp.float32),
+        ),
+        in_specs=[vmem],
+        out_specs=(vmem, vmem, vmem),
+        scratch_shapes=[
+            pltpu.VMEM((5, block, block), bf16),
+            pltpu.VMEM((5, inner - 1, slab, block), bf16),
+            pltpu.VMEM((5, slab, block), bf16),
+            pltpu.VMEM((5, outer - 1, piece, block), bf16),
+            pltpu.VMEM((2, 5, block, block), bf16),
+            pltpu.VMEM((states, states), bf16),
+            pltpu.VMEM((states, width), jnp.float32),
+            pltpu.VMEM((states, width), bf16),
+            pltpu.VMEM((states, width), bf16),
+            dma, dma,
+            dma((5, inner - 1)), dma((5, inner - 1)),
+            dma((5, outer - 1)), dma((5, outer - 1)),
+            dma((5, outer - 1)), dma((5, outer - 1)),
+            dma((5, inner - 1)), dma((5, inner - 1)),
+            dma((5,)), dma((5,)),
+        ],
+        compiler_params=pltpu.CompilerParams(
+            vmem_limit_bytes=VMEM_LIMIT, collective_id=1, has_side_effects=True
+        ),
+        name="margin_root",
+    )(rounded)
+
+
 def passed_along(value, axis, steps):
     count = lax.axis_size(axis)
     initial, last = (max(0, -steps), min(count, count - steps))
@@ -163,6 +388,9 @@
         following = 2.0 * (hamiltonian(current) - filter_center * current) / filter_half - previous
         previous, current = (current, following)
     rounded = current.astype(bf16)
+    if lax.axis_size("band") == 2 and min(split_domains(domains)) > 1 and band_width % (32 * domains) == 0:
+        everyone, change, scale = margin_root(rounded, domains)
+        return (current + dot32(everyone, change)) * scale[0, 0]
     everyone = lax.all_gather(rounded, "band", axis=1, tiled=True)
     partial = dot32(everyone, rounded, ((0,), (0,))) / (own * domains)
     tile = lax.psum_scatter(partial.astype(bf16), "dom", scatter_dimension=0, tiled=True)

time: 338 us -> 181 us (0.54); the launches traced: 332 us -> 181 us
  waiting for transfers between devices: 168 us -> 9.13 us
  Pallas kernels: 47.1 us -> 85.5 us
  between operations: 14.5 us -> 0.38 us
  matrix products: 56.1 us -> 43.6 us
  other arithmetic: 11.3 us -> 6.43 us
    reduce_scatter x1 -> x0, waiting for transfers between devices: 80 us -> none  [on_device(): lax.psum_scatter(partial.astype(bf16), 'dom', scatter_dimension=0, tiled=...]
    all_gather x3 -> x0, waiting for transfers between devices: 76.5 us -> none  [the longest x1 53.9 us: on_device(): columns = lax.all_gather(tile, 'dom', axis=0, tiled=True)]
    pallas_call x0 -> x1, Pallas kernels: none -> 38.1 us  [margin_root(): pl.pallas_call(functools.partial(margin_kernel, inner, outer), out_shape=...]
    dot_general x16 -> x13, matrix products: 56.1 us -> 43.6 us  [dot32(): lax.dot_general(a, b, (dims, ((), ())), preferred_element_type=jnp.float32)]
  transfers between devices with their start and end apart: 11 -> 7, of which waited for: 7 -> 3; matrix products, arithmetic and copies ran while one was open for 7% -> 14% of each run, Pallas kernels for 0% -> 0%
where the time goes in v1:
time: 181 us
  Pallas kernels  85.5 us (47%)
  matrix products  43.6 us (24%)
  starting transfers between devices  23.8 us (13%)
  local copies, waits for them, and re-layouts  11.9 us (7%)
  waiting for transfers between devices  9.13 us (5%)
  other arithmetic  6.43 us (4%)
    pallas_call x1, Pallas kernels, domain_operator(): pl.pallas_call(functools.partial(operator_kernel, share), out_shape=jax.S...  47.4 us
    dot_general x13, matrix products, dot32(): lax.dot_general(a, b, (dims, ((), ())), preferred_element_type=jnp.float32)  43.6 us
    pallas_call x1, Pallas kernels, margin_root(): pl.pallas_call(functools.partial(margin_kernel, inner, outer), out_shape=...  38.1 us
    ppermute x7, starting transfers between devices, passed_along(): lax.ppermute(value, axis, [(source, source + steps) for source in range(i...  23.8 us
    ppermute x7, waiting for transfers between devices, passed_along(): lax.ppermute(value, axis, [(source, source + steps) for source in range(i...  9.13 us
    squeeze x1, local copies, waits for them, and re-layouts, domain_operator(): halves[i, :, :width]  8.83 us
  transfers between devices with their start and end apart: 7, of which 3 were waited for; matrix products, arithmetic and copies ran while one was open for 14% of the time, Pallas kernels for 0%

profile of v1, /device:TPU:0, one launch (start us, length us, event | category | flops | bytes accessed | tf_op | source)
XLA Modules:
  0.0 180.8 jit_solution(5244895245471937043)
XLA Ops:
  0.0 47.4 %domain_operator.1 = bf16[2,2304,1280]{2,1,0:T(8,128)(2,1)} custom-call(s32[8,512]{1,0:T(8,128)} %conn_ref.1, bf16[8,512,512]{2,1,0:T(8,128)(2,1)} %a_ref.1), custom_call_target="tpu_custom_call" | custom-call | tf_op jit(solution)/shard_map/domain_operator/pallas_call | solution.py:105
  47.4 1.4 convert_add_fusion
  48.8 8.8 %slice_bitcast_fusion = (bf16[2304,1152]{1,0:T(8,128)(2,1)}, bf16[2304,1152]{1,0:T(8,128)(2,1)}) fusion(bf16[2,2304,1280]{2,1,0:T(8,128)(2,1)} %domain_operator.1), kind=kLoop, calls=%fused_computation.6 | loop fusion | bytes 21233664 | tf_op jit(solution)/shard_map/squeeze | solution.py:120
  57.6 0.9 slice.90
  58.6 4.8 %collective-permute-start.2 = (bf16[256,384]{1,0:T(8,128)(2,1)S(1)}, bf16[256,384]{1,0:T(8,128)(2,1)S(1)}, u32[]{:S(2)}, u32[]{:S(2)}) collective-permute-start(bf16[256,384]{1,0:T(8,128)(2,1)S(1)} %pad_maximum_fusion.5), channel_id=1, source_target_pairs={{0,2},{2,4},{4,6},{6,8},{8,10},{10,12},{12,14},{14,16},{16,18},{18... | collective-permute-start | bytes 589832 | tf_op jit(solution)/shard_map/ppermute | solution.py:351
  63.7 1.6 fusion.3
  65.3 0.4 copy-done.2
  65.7 1.4 convolution_convert_fusion.2
  67.1 1.4 collective-permute-start
  68.5 4.7 %collective-permute-start.1 = (bf16[256,512]{1,0:T(8,128)(2,1)S(1)}, bf16[256,512]{1,0:T(8,128)(2,1)S(1)}, u32[]{:S(2)}, u32[]{:S(2)}) collective-permute-start(bf16[256,512]{1,0:T(8,128)(2,1)S(1)} %get-tuple-element.22), channel_id=1, source_target_pairs={{0,2},{2,4},{4,6},{6,8},{8,10},{10,12},{12,14},{14,16},{16,18},{18... | collective-permute-start | bytes 786440 | tf_op jit(solution)/shard_map/ppermute | solution.py:351
  73.3 0.5 fusion.4
  73.8 1.4 fusion.46
  75.2 1.2 fusion
  76.4 4.6 %fusion.22 = f32[2048,512]{1,0:T(8,128)S(1)} fusion(bf16[2048,2048]{1,0:T(8,128)(2,1)S(1)} %fusion, bf16[2048,512]{1,0:T(8,128)(2,1)S(1)} %copy-done.2, f32[2048]{0:T(1024)S(1)} %copy-done), kind=kOutput, calls=%fused_computation.44 | convolution fusion | flops 4298113024 | bytes 14688256 | tf_op jit(solution)/shard_map/dot_general | solution.py:21
  81.1 0.3 slice_reduce_fusion
  81.6 2.1 %collective-permute-done.1 = bf16[256,512]{1,0:T(8,128)(2,1)S(1)} collective-permute-done((bf16[256,512]{1,0:T(8,128)(2,1)S(1)}, bf16[256,512]{1,0:T(8,128)(2,1)S(1)}, u32[]{:S(2)}, u32[]{:S(2)}) %collective-permute-start.1) | collective-permute-done | bytes 262176 | tf_op jit(solution)/shard_map/ppermute | solution.py:351
  84.0 2.5 %fusion.2 = f32[2048,512]{1,0:T(8,128)S(1)} fusion(bf16[2048,512]{1,0:T(8,128)(2,1)S(1)} %copy-done.2, f32[2048,512]{1,0:T(8,128)S(1)} %fusion.22, f32[2048]{0:T(1024)S(1)} %slice_reduce_fusion, f32[2048]{0:T(1024)S(1)} %copy-done, bf16[256,512]{1,0:T(8,128)(2,1)S(1)} %get-tuple-element.24, bf16[256,512]{1,0:T(8,128)(2,1)S(1)} %get-tuple-element.23, ...), kind=kOutput, calls=%fused_computation.9 | convolution fusion | flops 1632894976 | bytes 13385728 | tf_op jit(solution)/shard_map/dot_general | solution.py:21
  86.4 1.4 convolution_convert_fusion.1
  87.9 1.3 collective-permute-start.3
  89.2 5.3 %collective-permute-start.4 = (bf16[256,512]{1,0:T(8,128)(2,1)S(1)}, bf16[256,512]{1,0:T(8,128)(2,1)S(1)}, u32[]{:S(2)}, u32[]{:S(2)}) collective-permute-start(bf16[256,512]{1,0:T(8,128)(2,1)S(1)} %get-tuple-element.18), channel_id=1, source_target_pairs={{0,2},{2,4},{4,6},{6,8},{8,10},{10,12},{12,14},{14,16},{16,18},{18... | collective-permute-start | bytes 786440 | tf_op jit(solution)/shard_map/ppermute | solution.py:351
  94.4 6.2 %fusion.48 = f32[2048,512]{1,0:T(8,128)} fusion(bf16[2048,2048]{1,0:T(8,128)(2,1)S(1)} %fusion, f32[2048,512]{1,0:T(8,128)S(1)} %fusion.2, f32[2048]{0:T(1024)S(1)} %broadcast_multiply_fusion), kind=kOutput, calls=%fused_computation.70 | convolution fusion | flops 4297064448 | bytes 16785408 | tf_op jit(solution)/shard_map/dot_general | solution.py:21
  100.7 2.8 %collective-permute-done.4 = bf16[256,512]{1,0:T(8,128)(2,1)S(1)} collective-permute-done((bf16[256,512]{1,0:T(8,128)(2,1)S(1)}, bf16[256,512]{1,0:T(8,128)(2,1)S(1)}, u32[]{:S(2)}, u32[]{:S(2)}) %collective-permute-start.4) | collective-permute-done | bytes 262176 | tf_op jit(solution)/shard_map/ppermute | solution.py:351
  103.7 4.2 %convert_subtract_fusion = f32[2048,512]{1,0:T(8,128)S(1)} fusion(bf16[2048,512]{1,0:T(8,128)(2,1)S(1)} %copy-done.2, f32[2048,512]{1,0:T(8,128)S(1)} %fusion.2, f32[2048,512]{1,0:T(8,128)} %fusion.48, f32[2048]{0:T(1024)S(1)} %slice_reduce_fusion, f32[2048]{0:T(1024)S(1)} %copy-done, bf16[256,512]{1,0:T(8,128)(2,1)S(1)} %get-tuple-element.20, ...), kind=kOutput, calls=%fused_computation.3 | convolution fusion | flops 1633943552 | bytes 17588224 | tf_op jit(solution)/shard_map/dot_general | solution.py:21
  107.9 1.4 convolution_convert_fusion
  109.3 1.3 collective-permute-start.5
  110.6 5.0 %collective-permute-start.6 = (bf16[256,512]{1,0:T(8,128)(2,1)S(1)}, bf16[256,512]{1,0:T(8,128)(2,1)S(1)}, u32[]{:S(2)}, u32[]{:S(2)}) collective-permute-start(bf16[256,512]{1,0:T(8,128)(2,1)S(1)} %get-tuple-element.14), channel_id=1, source_target_pairs={{0,2},{2,4},{4,6},{6,8},{8,10},{10,12},{12,14},{14,16},{16,18},{18... | collective-permute-start | bytes 786440 | tf_op jit(solution)/shard_map/ppermute | solution.py:351
  115.7 6.3 %fusion.47 = f32[2048,512]{1,0:T(8,128)} fusion(bf16[2048,2048]{1,0:T(8,128)(2,1)S(1)} %fusion, f32[2048,512]{1,0:T(8,128)S(1)} %convert_subtract_fusion, f32[2048]{0:T(1024)S(1)} %copy-done), kind=kOutput, calls=%fused_computation.69 | convolution fusion | flops 4297064448 | bytes 16785408 | tf_op jit(solution)/shard_map/dot_general | solution.py:21
  121.9 4.3 %collective-permute-done.6 = bf16[256,512]{1,0:T(8,128)(2,1)S(1)} collective-permute-done((bf16[256,512]{1,0:T(8,128)(2,1)S(1)}, bf16[256,512]{1,0:T(8,128)(2,1)S(1)}, u32[]{:S(2)}, u32[]{:S(2)}) %collective-permute-start.6) | collective-permute-done | bytes 262176 | tf_op jit(solution)/shard_map/ppermute | solution.py:351
  126.5 6.1 %fusion.55 = (bf16[2048,512]{1,0:T(8,128)(2,1)}, f32[2048,512]{1,0:T(8,128)}) fusion(f32[2048,512]{1,0:T(8,128)S(1)} %fusion.2, f32[2048,512]{1,0:T(8,128)S(1)} %convert_subtract_fusion, bf16[256,512]{1,0:T(8,128)(2,1)S(1)} %get-tuple-element.16, bf16[256,512]{1,0:T(8,128)(2,1)S(1)} %get-tuple-element.15, bf16[256,512]{1,0:T(8,128)(2,1)S(1)} %collective-permute-done.5, ...), kind=kOutput, calls=%fused_computation.77 | convolution fusion | flops 1636040704 | bytes 21774336 | tf_op jit(solution)/shard_map/dot_general | solution.py:21
  132.6 38.1 %margin_root.1 = (bf16[2048,1024]{1,0:T(8,128)(2,1)}, bf16[1024,512]{1,0:T(8,128)(2,1)}, f32[8,128]{1,0:T(8,128)}) custom-call(bf16[2048,512]{1,0:T(8,128)(2,1)} %get-tuple-element.25.rounded_ref), custom_call_target="tpu_custom_call" | custom-call | tf_op jit(solution)/shard_map/margin_root/pallas_call | solution.py:315
  170.7 1.2 slice.83
  172.0 8.8 %add_multiply_fusion = f32[2048,512]{1,0:T(8,128)} fusion(f32[2048,512]{1,0:T(8,128)} %get-tuple-element.26, bf16[2048,1024]{1,0:T(8,128)(2,1)} %get-tuple-element.8, bf16[1024,512]{1,0:T(8,128)(2,1)} %get-tuple-element.9, f32[]{:T(128)} %bitcast.4), kind=kOutput, calls=%fused_computation.10 | convolution fusion | flops 2149580800 | bytes 13631492 | tf_op jit(solution)/shard_map/dot_general | solution.py:21
  (31 shorter events, 1.4 us)
Async XLA Ops:
  48.8 14.6 %copy-start.1 = (s32[256]{0:T(256)S(1)}, s32[256]{0:T(256)}, u32[]{:S(2)}) copy-start(s32[256]{0:T(256)} %param.9) | copy-start | bytes 3076
  58.6 22.9 %collective-permute-start.2 = (bf16[256,384]{1,0:T(8,128)(2,1)S(1)}, bf16[256,384]{1,0:T(8,128)(2,1)S(1)}, u32[]{:S(2)}, u32[]{:S(2)}) collective-permute-start(bf16[256,384]{1,0:T(8,128)(2,1)S(1)} %pad_maximum_fusion.5), channel_id=1, source_target_pairs={{0,2},{2,4},{4,6},{6,8},{8,10},{10,12},{12,14},{14,16},{16,18},{18... | collective-permute-start | bytes 589832 | tf_op jit(solution)/shard_map/ppermute | solution.py:351
  63.6 11.6 %slice-start = ((s8[5308416]{0:T(1024)(128)(4,1)}), s8[4194304]{0:T(1024)(128)(4,1)S(1)}, s32[]{:S(2)}) async-start(s8[5308416]{0:T(1024)(128)(4,1)} %bitcast.17), calls=%async_computation | async-start | bytes 8388608
  63.6 11.6 %slice-start.2 = ((s8[5308416]{0:T(1024)(128)(4,1)}), s8[4194304]{0:T(1024)(128)(4,1)S(1)}, s32[]{:S(2)}) async-start(s8[5308416]{0:T(1024)(128)(4,1)} %bitcast.19), calls=%async_computation.2 | async-start | bytes 8388608
  63.6 1.7 copy-start
  63.6 2.1 %copy-start.2 = (bf16[2048,512]{1,0:T(8,128)(2,1)S(1)}, bf16[2048,512]{1,0:T(8,128)(2,1)}, u32[]{:S(2)}) copy-start(bf16[2048,512]{1,0:T(8,128)(2,1)} %param.5) | copy-start | bytes 6291460
  63.6 11.6 %slice-start.1 = ((s8[5308416]{0:T(1024)(128)(4,1)}), s8[1114112]{0:T(1024)(128)(4,1)S(1)}, s32[]{:S(2)}) async-start(s8[5308416]{0:T(1024)(128)(4,1)} %bitcast.17), calls=%async_computation.1 | async-start | bytes 2228224
  63.7 11.6 %slice-start.3 = ((s8[5308416]{0:T(1024)(128)(4,1)}), s8[1114112]{0:T(1024)(128)(4,1)S(1)}, s32[]{:S(2)}) async-start(s8[5308416]{0:T(1024)(128)(4,1)} %bitcast.19), calls=%async_computation.3 | async-start | bytes 2228224
  67.1 16.8 %collective-permute-start = (bf16[256,512]{1,0:T(8,128)(2,1)S(1)}, bf16[256,512]{1,0:T(8,128)(2,1)S(1)}, u32[]{:S(2)}, u32[]{:S(2)}) collective-permute-start(bf16[256,512]{1,0:T(8,128)(2,1)S(1)} %get-tuple-element.21), channel_id=1, source_target_pairs={{2,0},{4,2},{6,4},{8,6},{10,8},{12,10},{14,12},{16,14},{18,16},{20... | collective-permute-start | bytes 786440 | tf_op jit(solution)/shard_map/ppermute | solution.py:351
  68.5 15.1 %collective-permute-start.1 = (bf16[256,512]{1,0:T(8,128)(2,1)S(1)}, bf16[256,512]{1,0:T(8,128)(2,1)S(1)}, u32[]{:S(2)}, u32[]{:S(2)}) collective-permute-start(bf16[256,512]{1,0:T(8,128)(2,1)S(1)} %get-tuple-element.22), channel_id=1, source_target_pairs={{0,2},{2,4},{4,6},{6,8},{8,10},{10,12},{12,14},{14,16},{16,18},{18... | collective-permute-start | bytes 786440 | tf_op jit(solution)/shard_map/ppermute | solution.py:351
  87.9 15.8 %collective-permute-start.3 = (bf16[256,512]{1,0:T(8,128)(2,1)S(1)}, bf16[256,512]{1,0:T(8,128)(2,1)S(1)}, u32[]{:S(2)}, u32[]{:S(2)}) collective-permute-start(bf16[256,512]{1,0:T(8,128)(2,1)S(1)} %get-tuple-element.17), channel_id=1, source_target_pairs={{2,0},{4,2},{6,4},{8,6},{10,8},{12,10},{14,12},{16,14},{18,16},{20... | collective-permute-start | bytes 786440 | tf_op jit(solution)/shard_map/ppermute | solution.py:351
  89.2 14.3 %collective-permute-start.4 = (bf16[256,512]{1,0:T(8,128)(2,1)S(1)}, bf16[256,512]{1,0:T(8,128)(2,1)S(1)}, u32[]{:S(2)}, u32[]{:S(2)}) collective-permute-start(bf16[256,512]{1,0:T(8,128)(2,1)S(1)} %get-tuple-element.18), channel_id=1, source_target_pairs={{0,2},{2,4},{4,6},{6,8},{8,10},{10,12},{12,14},{14,16},{16,18},{18... | collective-permute-start | bytes 786440 | tf_op jit(solution)/shard_map/ppermute | solution.py:351
  109.3 17.1 %collective-permute-start.5 = (bf16[256,512]{1,0:T(8,128)(2,1)S(1)}, bf16[256,512]{1,0:T(8,128)(2,1)S(1)}, u32[]{:S(2)}, u32[]{:S(2)}) collective-permute-start(bf16[256,512]{1,0:T(8,128)(2,1)S(1)} %get-tuple-element.13), channel_id=1, source_target_pairs={{2,0},{4,2},{6,4},{8,6},{10,8},{12,10},{14,12},{16,14},{18,16},{20... | collective-permute-start | bytes 786440 | tf_op jit(solution)/shard_map/ppermute | solution.py:351
  110.6 15.6 %collective-permute-start.6 = (bf16[256,512]{1,0:T(8,128)(2,1)S(1)}, bf16[256,512]{1,0:T(8,128)(2,1)S(1)}, u32[]{:S(2)}, u32[]{:S(2)}) collective-permute-start(bf16[256,512]{1,0:T(8,128)(2,1)S(1)} %get-tuple-element.14), channel_id=1, source_target_pairs={{0,2},{2,4},{4,6},{6,8},{8,10},{10,12},{12,14},{14,16},{16,18},{18... | collective-permute-start | bytes 786440 | tf_op jit(solution)/shard_map/ppermute | solution.py:351

commit v2 on v0

--- a/solution.py
+++ b/solution.py
@@ -11,6 +11,7 @@
 filter_half = 5.0
 MESH = pl.DeviceIdType.MESH
 VMEM_LIMIT = 62 * 1024 * 1024
+FUSED_LIMIT = 67043328
 
 
 def row_tile(rows, most):
@@ -120,6 +121,541 @@
     return jnp.concatenate([halves[i, :, :width] for i in range(share)], axis=1), rest
 
 
+def upper_blocks(band):
+    other = 1 - band
+    return (
+        (2 * band, 2 * band),
+        (2 * band, 2 * band + 1),
+        (2 * band + 1, 2 * band + 1),
+        (2 * band, 2 * other + band),
+        (2 * band + 1, 2 * other + 1 - band),
+    )
+
+
+def split_domains(domains):
+    inner = max(n for n in range(1, domains + 1) if domains % n == 0 and n * n <= domains)
+    return inner, domains // inner
+
+
+def column_form(row):
+    return jnp.broadcast_to(row, (128, 128)).T
+
+
+def one_hot(ids, links):
+    return jnp.where(ids == links, 1.0, 0.0).astype(jnp.bfloat16)
+
+
+def span(index, size):
+    return pl.ds(pl.multiple_of(index * size, size), size)
+
+
+def fused_kernel(inner, outer, names, *args):
+    refs = dict(zip(names, args))
+    conn_ref, a_ref, mass_ref, face_ref, wave_ref = (refs[n] for n in names[:5])
+    everyone_out, filtered_out, change_ref, scale_ref = (refs[n] for n in names[5:9])
+    matrix, b, picks, hits = (refs[n] for n in ("matrix", "b", "picks", "hits"))
+    mass_all, face_column, face_of, face_in = (
+        refs[n] for n in ("mass_all", "face_column", "face_of", "face_in")
+    )
+    scaled, sent, returned_in, faces_in, corner_in = (
+        refs[n] for n in ("scaled", "sent", "returned_in", "faces_in", "corner_in")
+    )
+    rests, rest_all, corner_rest, corner_rest_in, added_low = (
+        refs[n] for n in ("rests", "rest_all", "corner_rest", "corner_rest_in", "added_low")
+    )
+    states_one, states_two, everyone = (refs[n] for n in ("states_one", "states_two", "everyone"))
+    part, first_in, first_sum, second_in, gathered = (
+        refs[n] for n in ("part", "first_in", "first_sum", "second_in", "gathered")
+    )
+    offset, second, third, term = (refs[n] for n in ("offset", "second", "third", "term"))
+    bf16, f32 = jnp.bfloat16, jnp.float32
+    cells, nodes = conn_ref.shape
+    own, width = wave_ref.shape
+    face = face_ref.shape[1]
+    extent = own + face
+    states, block = 2 * width, width // 2
+    share = extent // 2
+    domains = inner * outer
+    slab, piece = block // inner, block // inner // outer
+    chunks = 5
+    me = lax.axis_index("band")
+    dom = lax.axis_index("dom")
+    high, low = dom // inner, lax.rem(dom, inner)
+    partner = 1 - me
+    after, before = lax.rem(dom + 1, domains), lax.rem(dom + domains - 1, domains)
+    plane = [high * inner + lax.rem(low + step, inner) for step in range(1, inner)]
+    line = [lax.rem(high + step, outer) * inner + low for step in range(1, outer)]
+    has_after, has_before = dom < domains - 1, dom > 0
+
+    barrier = pltpu.get_barrier_semaphore()
+    for peer in plane + line + [after, before]:
+        pl.semaphore_signal(barrier, inc=1, device_id={"dom": peer}, device_id_type=MESH)
+    pl.semaphore_signal(barrier, inc=1, device_id={"band": partner}, device_id_type=MESH)
+
+    def remote(source, target, name, *at, **where):
+        return pltpu.make_async_remote_copy(
+            src_ref=source, dst_ref=target,
+            send_sem=refs[name + "_send"].at[at], recv_sem=refs[name + "_recv"].at[at],
+            device_id=where, device_id_type=MESH,
+        )
+
+    @pl.loop(0, own // 128)
+    def _(i):
+        mass_all[span(i, 128), :] = column_form(mass_ref[:, span(i, 128)])
+
+    for i in range(face // 128):
+        face_column[i * 128 : (i + 1) * 128, :] = column_form(
+            face_ref[:, i * 128 : (i + 1) * 128].astype(f32)
+        ).astype(jnp.int32)
+
+    @pl.loop(0, own // 128)
+    def _(i):
+        ids = lax.broadcasted_iota(jnp.int32, (face, 128), 1) + i * 128
+        face_of[:, span(i, 128)] = one_hot(ids, face_column[...])
+        ids = lax.broadcasted_iota(jnp.int32, (128, face), 0) + i * 128
+        face_in[span(i, 128), :] = one_hot(ids, face_ref[...])
+
+    def wide(value):
+        return jnp.concatenate([value] * (block // 128), axis=1)
+
+    def mass_tile(rows):
+        return wide(mass_all[rows, :])
+
+    @pl.loop(0, own // face)
+    def _(t):
+        rows = span(t, face)
+        for h in range(2):
+            value = wave_ref[rows, h * block : (h + 1) * block].astype(f32)
+            scaled[h, rows, :] = (mass_tile(rows) * value).astype(bf16)
+
+    for k in range(3):
+        for h in range(2):
+            @pl.when(jnp.logical_not(has_after))
+            def _():
+                faces_in[k, h] = jnp.zeros_like(faces_in[k, h])
+
+            @pl.when(jnp.logical_not(has_before))
+            def _():
+                returned_in[k, h] = jnp.zeros_like(returned_in[k, h])
+
+    @pl.when(jnp.logical_not(has_before))
+    def _():
+        corner_in[...] = jnp.zeros_like(corner_in)
+        corner_rest_in[...] = jnp.zeros_like(corner_rest_in)
+
+    def face_copy(k, h):
+        return remote(sent.at[k, h, pl.ds(face, face)], faces_in.at[k, h], "face", k, h, dom=before)
+
+    def return_copy(k, h):
+        return remote(sent.at[k, h, pl.ds(0, face)], returned_in.at[k, h], "return", k, h, dom=after)
+
+    def corner_copy():
+        source = matrix.at[pl.ds(own, face), pl.ds(own, face)]
+        return remote(source, corner_in, "corner", 0, dom=after)
+
+    def corner_rest_copy():
+        return remote(corner_rest, corner_rest_in, "corner", 1, dom=after)
+
+    def send_faces(k, h):
+        sent[k, h, face:] = dot32(face_of[...], scaled[h]).astype(bf16)
+
+        @pl.when(has_before)
+        def _():
+            face_copy(k, h).start()
+
+    def send_returned(k, h):
+        sent[k, h, :face] = dot32(matrix[own:, :own], scaled[h]).astype(bf16)
+
+        @pl.when(has_after)
+        def _():
+            return_copy(k, h).start()
+
+    pl.semaphore_wait(barrier, inner + outer + 1)
+    for h in range(2):
+        send_faces(0, h)
+
+    columns = pl.ds(pl.multiple_of(me * share, 128), share)
+
+    @pl.loop(0, cells)
+    def _(c):
+        links = conn_ref[pl.ds(c, 1), :]
+
+        @pl.loop(0, share // 128)
+        def _(r):
+            ids = lax.broadcasted_iota(jnp.int32, (128, nodes), 0) + (r * 128 + me * share)
+            picks[span(r, 128), :] = one_hot(ids, links)
+
+        b[span(c, nodes), :] = dot32(a_ref[c], picks[...], ((1,), (1,))).astype(bf16)
+
+    tiles = extent // face
+
+    def matrix_copy(r):
+        spot = matrix.at[span(tiles - 1 - r, face), columns]
+        return remote(spot, spot, "matrix", r, band=partner)
+
+    def rest_copy(r):
+        spot = rests.at[me, span(tiles - 1 - r, face)]
+        return remote(spot, spot, "rest", r, band=partner)
+
+    @pl.loop(0, tiles)
+    def _(r):
+        t = tiles - 1 - r
+        for c in range(cells):
+            ids = lax.broadcasted_iota(jnp.int32, (face, nodes), 0) + t * face
+            hits[:, c * nodes : (c + 1) * nodes] = one_hot(ids, conn_ref[c : c + 1, :])
+        total = dot32(hits[...], b[...])
+        kept = total.astype(bf16)
+        matrix[span(t, face), columns] = kept
+        gaps = lax.broadcasted_iota(jnp.int32, (face, share), 1) - lax.broadcasted_iota(
+            jnp.int32, (face, share), 0
+        )
+        rest = jnp.where(gaps == t * face - me * share, total - kept.astype(f32), 0.0)
+        rest = jnp.sum(rest, axis=1, keepdims=True)
+        rests[me, span(t, face), :] = jnp.broadcast_to(rest, (face, 128)).astype(bf16)
+        matrix_copy(r).start()
+        rest_copy(r).start()
+
+        @pl.when(r == 1)
+        def _():
+            matrix_copy(0).wait()
+            rest_copy(0).wait()
+            corner_rest[...] = rests[0, own:, :] + rests[1, own:, :]
+
+            @pl.when(has_after)
+            def _():
+                corner_copy().start()
+                corner_rest_copy().start()
+
+            for h in range(2):
+                send_returned(0, h)
+
+    @pl.loop(1, tiles)
+    def _(r):
+        matrix_copy(r).wait()
+        rest_copy(r).wait()
+
+    @pl.loop(0, own // face)
+    def _(t):
+        rows = span(t, face)
+        rest_all[rows, :] = rests[0, rows, :].astype(f32) + rests[1, rows, :].astype(f32)
+
+    ratio = 1.0 / filter_half
+    shift = filter_center / filter_half
+
+    def wave_tile(h, rows):
+        return wave_ref[rows, h * block : (h + 1) * block].astype(f32)
+
+    def advance(k, h):
+        target = states_two if k == 1 else states_one
+
+        @pl.loop(0, own // face)
+        def _(t):
+            rows = span(t, face)
+            value = dot32(matrix[rows, :own], scaled[h])
+            value = value + wide(rest_all[rows, :]) * scaled[h, rows, :].astype(f32)
+            value = value * mass_tile(rows)
+            if k == 0:
+                target[h, rows, :] = ratio * value - shift * wave_tile(h, rows)
+            elif k == 1:
+                target[h, rows, :] = (
+                    2.0 * ratio * value - 2.0 * shift * states_one[h, rows, :] - wave_tile(h, rows)
+                )
+            else:
+                target[h, rows, :] = (
+                    2.0 * ratio * value - 2.0 * shift * states_two[h, rows, :] - states_one[h, rows, :]
+                )
+
+        def wait_both(copies):
+            for copy, sends, receives in copies:
+                @pl.when(sends)
+                def _():
+                    copy.wait_send()
+
+                @pl.when(receives)
+                def _():
+                    copy.wait_recv()
+
+        waits = [(face_copy(k, h), has_before, has_after), (return_copy(k, h), has_after, has_before)]
+        if k == 0 and h == 0:
+            waits.append((corner_copy(), has_after, has_before))
+            waits.append((corner_rest_copy(), has_after, has_before))
+        wait_both(waits)
+        added = returned_in[k, h].astype(f32) + dot32(corner_in[...], sent[k, h, face:])
+        added = added + wide(corner_rest_in[...].astype(f32)) * sent[k, h, face:].astype(f32)
+        kept = added.astype(bf16)
+        sent[k, h, :face] = kept
+        added_low[...] = (added - kept.astype(f32)).astype(bf16)
+        scale = ratio if k == 0 else 2.0 * ratio
+
+        @pl.loop(0, own // face)
+        def _(t):
+            rows = span(t, face)
+            value = dot32(matrix[rows, own:], faces_in[k, h]) + dot32(face_in[rows, :], sent[k, h, :face])
+            value = value + dot32(face_in[rows, :], added_low[...])
+            mass = mass_tile(rows)
+            value = target[h, rows, :] + scale * value * mass
+            target[h, rows, :] = value
+            if k < 2:
+                scaled[h, rows, :] = (mass * value).astype(bf16)
+            else:
+                everyone[2 * me + h, rows, :] = value.astype(bf16)
+
+    def band_copy(h):
+        spot = everyone.at[2 * me + h]
+        return remote(spot, spot, "band", h, band=partner)
+
+    def local(source, target, index):
+        return pltpu.make_async_copy(source, target, refs["local_sem"].at[index])
+
+    def filtered_copy(h):
+        return local(states_one.at[h], filtered_out.at[h], h)
+
+    def everyone_copy(i):
+        q = 2 * me + i if i < 2 else 2 * partner + i - 2
+        return local(everyone.at[q], everyone_out.at[q], 2 + i)
+
+    def plane_copies(c):
+        return [
+            remote(
+                part.at[c, span(lax.rem(low + step, inner), slab)],
+                first_in.at[c, step - 1], "one", c, step - 1, dom=plane[step - 1],
+            )
+            for step in range(1, inner)
+        ]
+
+    def line_copies(c):
+        return [
+            remote(
+                first_sum.at[c, span(lax.rem(high + step, outer), piece)],
+                second_in.at[c, step - 1], "two", c, step - 1, dom=line[step - 1],
+            )
+            for step in range(1, outer)
+        ]
+
+    own_slab = span(low, slab)
+    own_piece = pl.ds(pl.multiple_of(low * slab + high * piece, piece), piece)
+
+    def line_back(c):
+        spot = gathered.at[me, c, own_piece]
+        return [remote(spot, spot, "three", c, s - 1, dom=line[s - 1]) for s in range(1, outer)]
+
+    def plane_back(c):
+        spot = gathered.at[me, c, own_slab]
+        return [remote(spot, spot, "four", c, s - 1, dom=plane[s - 1]) for s in range(1, inner)]
+
+    def band_back(c):
+        spot = gathered.at[me, c]
+        return remote(spot, spot, "five", c, band=partner)
+
+    def emit(c, left, right):
+        value = dot32(everyone[left], everyone[right], ((0,), (0,)))
+        part[c] = (value * (1.0 / (own * domains))).astype(bf16)
+        for copy in plane_copies(c):
+            copy.start()
+
+    for k in range(3):
+        for h in range(2):
+            advance(k, h)
+            if k < 2:
+                send_faces(k + 1, h)
+                send_returned(k + 1, h)
+            else:
+                band_copy(h).start()
+                filtered_copy(h).start()
+                everyone_copy(h).start()
+                if h == 0:
+                    emit(0, 2 * me, 2 * me)
+    emit(1, 2 * me, 2 * me + 1)
+    emit(2, 2 * me + 1, 2 * me + 1)
+    for h in range(2):
+        band_copy(h).wait()
+        everyone_copy(2 + h).start()
+    for i in range(2):
+        emit(3 + i, 2 * me + i, 2 * partner + i + me - 2 * i * me)
+
+    for c in range(chunks):
+        total = part[c, own_slab].astype(f32)
+        for step, copy in enumerate(plane_copies(c)):
+            copy.wait()
+            total = total + first_in[c, step].astype(f32)
+        first_sum[c] = total.astype(bf16)
+        for copy in line_copies(c):
+            copy.start()
+    for c in range(chunks):
+        total = first_sum[c, span(high, piece)].astype(f32)
+        for step, copy in enumerate(line_copies(c)):
+            copy.wait()
+            total = total + second_in[c, step].astype(f32)
+        gathered[me, c, own_piece] = total.astype(bf16)
+        for copy in line_back(c):
+            copy.start()
+    for c in range(chunks):
+        for copy in line_back(c):
+            copy.wait()
+        for copy in plane_back(c):
+            copy.start()
+    for c in range(chunks):
+        for copy in plane_back(c):
+            copy.wait()
+        band_back(c).start()
+    for c in range(chunks):
+        band_back(c).wait()
+
+    unit = (
+        lax.broadcasted_iota(jnp.int32, (block, block), 0)
+        == lax.broadcasted_iota(jnp.int32, (block, block), 1)
+    ).astype(f32)
+    trace = 0.0
+    for q in range(2):
+        for c in (0, 2):
+            trace = trace + jnp.sum(gathered[q, c].astype(f32) * unit)
+    mean_eigen = jnp.full((1, 1), trace, f32) / states
+    inverse = 1.0 / mean_eigen
+    scale_ref[...] = jnp.broadcast_to(lax.rsqrt(mean_eigen), scale_ref.shape)
+    for q in range(2):
+        for c, (i, j) in enumerate(upper_blocks(q)):
+            value = gathered[q, c].astype(f32) * inverse
+            if i == j:
+                value = value - unit
+            offset[i * block : (i + 1) * block, j * block : (j + 1) * block] = value.astype(bf16)
+            if i != j:
+                offset[j * block : (j + 1) * block, i * block : (i + 1) * block] = value.T.astype(bf16)
+
+    mine = pl.ds(pl.multiple_of(me * width, 128), width)
+
+    @pl.loop(0, states // block)
+    def _(r):
+        rows = span(r, block)
+        value = dot32(offset[rows, :], offset[:, mine])
+        second[rows, :] = value
+        term[rows, :] = value.astype(bf16)
+
+    @pl.loop(0, states // block)
+    def _(r):
+        rows = span(r, block)
+        value = dot32(offset[rows, :], term[...])
+        third[rows, :] = (value / 16.0 - second[rows, :] * (5.0 / 16.0)).astype(bf16)
+
+    @pl.loop(0, states // block)
+    def _(r):
+        rows = span(r, block)
+        tail = dot32(offset[rows, :], third[...])
+        first = offset[rows, mine].astype(f32)
+        change_ref[rows, :] = (tail + 0.375 * second[rows, :] - 0.5 * first).astype(bf16)
+
+    for h in range(2):
+        filtered_copy(h).wait()
+    for i in range(4):
+        everyone_copy(i).wait()
+
+
+def rotate_kernel(filtered_ref, everyone_ref, change_ref, scale_ref, out_ref):
+    block = everyone_ref.shape[2]
+    value = jnp.concatenate([filtered_ref[0], filtered_ref[1]], axis=1)
+    for q in range(4):
+        value = value + dot32(everyone_ref[q], change_ref[q * block : (q + 1) * block, :])
+    out_ref[...] = value * scale_ref[0:1, 0:1]
+
+
+def fused(wavefunctions, mass_scale, cell_matrices, connectivity, face_index, domains):
+    bf16, f32 = jnp.bfloat16, jnp.float32
+    own, width = wavefunctions.shape
+    face = face_index.shape[0]
+    cells, nodes = connectivity.shape
+    extent, share = own + face, (own + face) // 2
+    states, block = 2 * width, width // 2
+    inner, outer = split_domains(domains)
+    slab = block // inner
+    piece = slab // outer
+    vmem = pl.BlockSpec(memory_space=pltpu.VMEM)
+    hbm = pl.BlockSpec(memory_space=pl.ANY)
+    dma = pltpu.SemaphoreType.DMA
+    scratch = dict(
+        matrix=pltpu.VMEM((extent, extent), bf16),
+        b=pltpu.VMEM((cells * nodes, share), bf16),
+        picks=pltpu.VMEM((share, nodes), bf16),
+        hits=pltpu.VMEM((face, cells * nodes), bf16),
+        mass_all=pltpu.VMEM((own, 128), f32),
+        face_column=pltpu.VMEM((face, 128), jnp.int32),
+        face_of=pltpu.VMEM((face, own), bf16),
+        face_in=pltpu.VMEM((own, face), bf16),
+        scaled=pltpu.VMEM((2, own, block), bf16),
+        sent=pltpu.VMEM((3, 2, 2 * face, block), bf16),
+        returned_in=pltpu.VMEM((3, 2, face, block), bf16),
+        faces_in=pltpu.VMEM((3, 2, face, block), bf16),
+        corner_in=pltpu.VMEM((face, face), bf16),
+        rests=pltpu.VMEM((2, extent, 128), bf16),
+        rest_all=pltpu.VMEM((own, 128), f32),
+        corner_rest=pltpu.VMEM((face, 128), bf16),
+        corner_rest_in=pltpu.VMEM((face, 128), bf16),
+        added_low=pltpu.VMEM((face, block), bf16),
+        states_one=pltpu.VMEM((2, own, block), f32),
+        states_two=pltpu.VMEM((2, own, block), f32),
+        everyone=pltpu.VMEM((4, own, block), bf16),
+        part=pltpu.VMEM((5, block, block), bf16),
+        first_in=pltpu.VMEM((5, inner - 1, slab, block), bf16),
+        first_sum=pltpu.VMEM((5, slab, block), bf16),
+        second_in=pltpu.VMEM((5, outer - 1, piece, block), bf16),
+        gathered=pltpu.VMEM((2, 5, block, block), bf16),
+        offset=pltpu.VMEM((states, states), bf16),
+        second=pltpu.VMEM((states, width), f32),
+        third=pltpu.VMEM((states, width), bf16),
+        term=pltpu.VMEM((states, width), bf16),
+        local_sem=dma((6,)),
+    )
+    counts = dict(
+        face=(3, 2), corner=(2,), matrix=(extent // face,), rest=(extent // face,), band=(2,),
+        one=(5, inner - 1), two=(5, outer - 1), three=(5, outer - 1), four=(5, inner - 1), five=(5,),
+    )
+    counts["return"] = (3, 2)
+    for name, shape in counts.items():
+        scratch[name + "_send"] = dma(shape)
+        scratch[name + "_recv"] = dma(shape)
+    names = ("conn", "a", "mass", "face", "wave", "everyone_out", "filtered_out", "change", "scale")
+    everyone, filtered, change, scale = pl.pallas_call(
+        functools.partial(fused_kernel, inner, outer, names + tuple(scratch)),
+        out_shape=(
+            jax.ShapeDtypeStruct((4, own, block), bf16),
+            jax.ShapeDtypeStruct((2, own, block), f32),
+            jax.ShapeDtypeStruct((states, width), bf16),
+            jax.ShapeDtypeStruct((8, 128), f32),
+        ),
+        in_specs=[vmem] * 5,
+        out_specs=(hbm, hbm, vmem, vmem),
+        scratch_shapes=list(scratch.values()),
+        compiler_params=pltpu.CompilerParams(
+            vmem_limit_bytes=FUSED_LIMIT, collective_id=1, has_side_effects=True
+        ),
+        name="fused",
+    )(connectivity, cell_matrices, mass_scale[None, :], face_index[None, :], wavefunctions)
+    tile = face
+    return pl.pallas_call(
+        rotate_kernel,
+        grid=(own // tile,),
+        out_shape=jax.ShapeDtypeStruct((own, width), f32),
+        in_specs=[
+            pl.BlockSpec((2, tile, block), lambda i: (0, i, 0)),
+            pl.BlockSpec((4, tile, block), lambda i: (0, i, 0)),
+            pl.BlockSpec((states, width), lambda i: (0, 0)),
+            pl.BlockSpec((8, 128), lambda i: (0, 0)),
+        ],
+        out_specs=pl.BlockSpec((tile, width), lambda i: (i, 0)),
+        name="rotate",
+    )(filtered, everyone, change, scale)
+
+
+def fits(own, width, face, domains):
+    return (
+        lax.axis_size("band") == 2
+        and min(split_domains(domains)) > 1
+        and width % (32 * domains) == 0
+        and width % 256 == 0
+        and face % 128 == 0
+        and own % face == 0
+        and (own + face) % 256 == 0
+    )
+
+
 def passed_along(value, axis, steps):
     count = lax.axis_size(axis)
     initial, last = (max(0, -steps), min(count, count - steps))
@@ -132,6 +668,8 @@
     face = face_index.shape[0]
     domains = lax.axis_size("dom")
     states = band_width * lax.axis_size("band")
+    if fits(own, band_width, face, domains):
+        return fused(wavefunctions, mass_scale, cell_matrices, connectivity, face_index, domains)
     matrix, rest = domain_operator(cell_matrices, connectivity, own + face)
     face_of = (face_index[:, None] == lax.broadcasted_iota(jnp.int32, (face, own), 1)).astype(bf16)
     face_in = (face_index[None, :] == lax.broadcasted_iota(jnp.int32, (own, face), 0)).astype(bf16)

time: 338 us -> 133 us (0.39); the launches traced: 332 us -> 132 us
  waiting for transfers between devices: 168 us -> 0 us
  Pallas kernels: 47.1 us -> 132 us
  matrix products: 56.1 us -> 0 us
  starting transfers between devices: 24.7 us -> 0 us
  between operations: 14.5 us -> 0.01 us
  other arithmetic: 11.3 us -> 0 us
  local copies, waits for them, and re-layouts: 10.8 us -> 0 us
    pallas_call x1 -> x2, Pallas kernels: 47.1 us -> 132 us  [the longest x1 123 us: fused(): pl.pallas_call(functools.partial(fused_kernel, inner, outer, names + tupl...]
    reduce_scatter x1 -> x0, waiting for transfers between devices: 80 us -> none  [on_device(): lax.psum_scatter(partial.astype(bf16), 'dom', scatter_dimension=0, tiled=...]
    all_gather x3 -> x0, waiting for transfers between devices: 76.5 us -> none  [the longest x1 53.9 us: on_device(): columns = lax.all_gather(tile, 'dom', axis=0, tiled=True)]
    dot_general x16 -> x0, matrix products: 56.1 us -> none  [dot32(): lax.dot_general(a, b, (dims, ((), ())), preferred_element_type=jnp.float32)]
    ppermute x7 -> x0, starting transfers between devices: 24.3 us -> none  [passed_along(): lax.ppermute(value, axis, [(source, source + steps) for source in range(i...]
    ppermute x7 -> x0, waiting for transfers between devices: 11.4 us -> none  [passed_along(): lax.ppermute(value, axis, [(source, source + steps) for source in range(i...]
    squeeze x1 -> x0, local copies, waits for them, and re-layouts: 8.85 us -> none  [domain_operator(): halves[i, :, :width]]
  transfers between devices with their start and end apart: 11 -> 0, of which waited for: 7 -> 0; matrix products, arithmetic and copies ran while one was open for 7% -> 0% of each run, Pallas kernels for 0% -> 0%
where the time goes in v2:
time: 133 us; the launch traced here: 132 us
  Pallas kernels  132 us (99%)
    pallas_call x1, Pallas kernels, fused(): pl.pallas_call(functools.partial(fused_kernel, inner, outer, names + tupl...  123 us
    pallas_call x1, Pallas kernels, fused(): pl.pallas_call(rotate_kernel, grid=(own // tile,), out_shape=jax.ShapeDty...  9.17 us

profile of v2, /device:TPU:0, one launch (start us, length us, event | category | flops | bytes accessed | tf_op | source)
XLA Modules:
  0.0 132.5 jit_solution(2384218977879569841)
XLA Ops:
  0.0 123.3 %fused.1 = (bf16[4,2048,256]{2,1,0:T(8,128)(2,1)}, f32[2,2048,256]{2,1,0:T(8,128)}, bf16[1024,512]{1,0:T(8,128)(2,1)}, f32[8,128]{1,0:T(8,128)}) custom-call(s32[8,512]{1,0:T(8,128)} %args_0_.4, bf16[8,512,512]{2,1,0:T(8,128)(2,1)} %args_1_.4, f32[1,2048]{1,0:T(1,128)} %bitcast.2, s32[1,256]{1,0:T(1,128)} %bitcast.3, bf16[2048,512]{1,0:T(8,128)(2,1)} %args_4_.4), custom_call_target="tpu_custom_call" | custom-call | tf_op jit(solution)/shard_map/fused/pallas_call | solution.py:615
  123.3 9.2 %rotate.1 = f32[2048,512]{1,0:T(8,128)} custom-call(f32[2,2048,256]{2,1,0:T(8,128)} %get-tuple-element.9.filtered_ref, bf16[4,2048,256]{2,1,0:T(8,128)(2,1)} %get-tuple-element.10.everyone_ref, bf16[1024,512]{1,0:T(8,128)(2,1)} %get-tuple-element.11.change_ref, f32[8,128]{1,0:T(8,128)} %get-tuple-element.12.scale_ref), custom_call_target="tpu_custom_call" | custom-call | tf_op jit(solution)/shard_map/rotate/pallas_call | solution.py:632

commit v3 on v2

--- a/solution.py
+++ b/solution.py
@@ -152,14 +152,17 @@
 def fused_kernel(inner, outer, names, *args):
     refs = dict(zip(names, args))
     conn_ref, a_ref, mass_ref, face_ref, wave_ref = (refs[n] for n in names[:5])
-    everyone_out, filtered_out, change_ref, scale_ref = (refs[n] for n in names[5:9])
-    matrix, b, picks, hits = (refs[n] for n in ("matrix", "b", "picks", "hits"))
+    out_ref, change = refs[names[5]], refs["term"]
+    matrix, b, picks, picks_next, hits = (
+        refs[n] for n in ("matrix", "b", "picks", "picks_next", "hits")
+    )
     mass_all, face_column, face_of, face_in = (
         refs[n] for n in ("mass_all", "face_column", "face_of", "face_in")
     )
     scaled, sent, returned_in, faces_in, corner_in = (
         refs[n] for n in ("scaled", "sent", "returned_in", "faces_in", "corner_in")
     )
+    lost = refs["lost"]
     rests, rest_all, corner_rest, corner_rest_in, added_low = (
         refs[n] for n in ("rests", "rest_all", "corner_rest", "corner_rest_in", "added_low")
     )
@@ -276,16 +279,39 @@
 
     columns = pl.ds(pl.multiple_of(me * share, 128), share)
 
-    @pl.loop(0, cells)
-    def _(c):
-        links = conn_ref[pl.ds(c, 1), :]
-
-        @pl.loop(0, share // 128)
-        def _(r):
-            ids = lax.broadcasted_iota(jnp.int32, (128, nodes), 0) + (r * 128 + me * share)
-            picks[span(r, 128), :] = one_hot(ids, links)
-
-        b[span(c, nodes), :] = dot32(a_ref[c], picks[...], ((1,), (1,))).astype(bf16)
+    def pick(target, c):
+        links = conn_ref[pl.ds(c, 1), :].astype(f32)
+        for i in range(nodes // 128):
+            rows = slice(i * 128, (i + 1) * 128)
+            numbers = column_form(links[:, rows]).astype(jnp.int32)
+            for j in range(share // 128):
+                ids = lax.broadcasted_iota(jnp.int32, (128, 128), 1) + (j * 128 + me * share)
+                target[rows, j * 128 : (j + 1) * 128] = one_hot(ids, numbers)
+
+    def cell(c, picked):
+        half = nodes // 2
+        for i in range(2):
+            rows = slice(i * half, (i + 1) * half)
+            value = dot32(a_ref[c, rows, :], picked[...])
+            kept = value.astype(bf16)
+            b[pl.ds(pl.multiple_of(c * nodes + i * half, half), half), :] = kept
+            left = (value - kept.astype(f32)) * picked[rows, :].astype(f32)
+            lost[...] += jnp.sum(left.reshape(half // 8, 8, share), axis=0)
+
+    pick(picks, 0)
+    lost[...] = jnp.zeros_like(lost)
+
+    @pl.loop(0, cells // 2)
+    def _(g):
+        pick(picks_next, 2 * g + 1)
+        cell(2 * g, picks)
+        pick(picks, jnp.minimum(2 * g + 2, cells - 1))
+        cell(2 * g + 1, picks_next)
+
+    rest_all[...] = jnp.zeros_like(rest_all)
+    for j in range(share // 128):
+        row = jnp.sum(lost[:, j * 128 : (j + 1) * 128], axis=0, keepdims=True)
+        rest_all[pl.ds(pl.multiple_of(me * share + j * 128, 128), 128), :] = column_form(row)
 
     tiles = extent // face
 
@@ -311,7 +337,7 @@
         )
         rest = jnp.where(gaps == t * face - me * share, total - kept.astype(f32), 0.0)
         rest = jnp.sum(rest, axis=1, keepdims=True)
-        rests[me, span(t, face), :] = jnp.broadcast_to(rest, (face, 128)).astype(bf16)
+        rests[me, span(t, face), :] = (rest + rest_all[span(t, face), :]).astype(bf16)
         matrix_copy(r).start()
         rest_copy(r).start()
 
@@ -339,6 +365,7 @@
         rows = span(t, face)
         rest_all[rows, :] = rests[0, rows, :].astype(f32) + rests[1, rows, :].astype(f32)
 
+    tall = own // max(1, own // (2 * face))
     ratio = 1.0 / filter_half
     shift = filter_center / filter_half
 
@@ -348,9 +375,9 @@
     def advance(k, h):
         target = states_two if k == 1 else states_one
 
-        @pl.loop(0, own // face)
+        @pl.loop(0, own // tall)
         def _(t):
-            rows = span(t, face)
+            rows = span(t, tall)
             value = dot32(matrix[rows, :own], scaled[h])
             value = value + wide(rest_all[rows, :]) * scaled[h, rows, :].astype(f32)
             value = value * mass_tile(rows)
@@ -387,9 +414,9 @@
         added_low[...] = (added - kept.astype(f32)).astype(bf16)
         scale = ratio if k == 0 else 2.0 * ratio
 
-        @pl.loop(0, own // face)
+        @pl.loop(0, own // tall)
         def _(t):
-            rows = span(t, face)
+            rows = span(t, tall)
             value = dot32(matrix[rows, own:], faces_in[k, h]) + dot32(face_in[rows, :], sent[k, h, :face])
             value = value + dot32(face_in[rows, :], added_low[...])
             mass = mass_tile(rows)
@@ -407,12 +434,9 @@
     def local(source, target, index):
         return pltpu.make_async_copy(source, target, refs["local_sem"].at[index])
 
-    def filtered_copy(h):
-        return local(states_one.at[h], filtered_out.at[h], h)
-
-    def everyone_copy(i):
-        q = 2 * me + i if i < 2 else 2 * partner + i - 2
-        return local(everyone.at[q], everyone_out.at[q], 2 + i)
+    def out_copy(t, h):
+        target = out_ref.at[span(t, face), pl.ds(h * block, block)]
+        return local(states_two.at[h, span(t, face)], target, 2 * t + h)
 
     def plane_copies(c):
         return [
@@ -461,15 +485,12 @@
                 send_returned(k + 1, h)
             else:
                 band_copy(h).start()
-                filtered_copy(h).start()
-                everyone_copy(h).start()
                 if h == 0:
                     emit(0, 2 * me, 2 * me)
     emit(1, 2 * me, 2 * me + 1)
     emit(2, 2 * me + 1, 2 * me + 1)
     for h in range(2):
         band_copy(h).wait()
-        everyone_copy(2 + h).start()
     for i in range(2):
         emit(3 + i, 2 * me + i, 2 * partner + i + me - 2 * i * me)
 
@@ -511,7 +532,7 @@
             trace = trace + jnp.sum(gathered[q, c].astype(f32) * unit)
     mean_eigen = jnp.full((1, 1), trace, f32) / states
     inverse = 1.0 / mean_eigen
-    scale_ref[...] = jnp.broadcast_to(lax.rsqrt(mean_eigen), scale_ref.shape)
+    scale = lax.rsqrt(mean_eigen)
     for q in range(2):
         for c, (i, j) in enumerate(upper_blocks(q)):
             value = gathered[q, c].astype(f32) * inverse
@@ -541,20 +562,23 @@
         rows = span(r, block)
         tail = dot32(offset[rows, :], third[...])
         first = offset[rows, mine].astype(f32)
-        change_ref[rows, :] = (tail + 0.375 * second[rows, :] - 0.5 * first).astype(bf16)
-
-    for h in range(2):
-        filtered_copy(h).wait()
-    for i in range(4):
-        everyone_copy(i).wait()
-
-
-def rotate_kernel(filtered_ref, everyone_ref, change_ref, scale_ref, out_ref):
-    block = everyone_ref.shape[2]
-    value = jnp.concatenate([filtered_ref[0], filtered_ref[1]], axis=1)
-    for q in range(4):
-        value = value + dot32(everyone_ref[q], change_ref[q * block : (q + 1) * block, :])
-    out_ref[...] = value * scale_ref[0:1, 0:1]
+        change[rows, :] = (tail + 0.375 * second[rows, :] - 0.5 * first).astype(bf16)
+
+    @pl.loop(0, own // face)
+    def _(t):
+        rows = span(t, face)
+        value = jnp.concatenate([states_one[0, rows, :], states_one[1, rows, :]], axis=1)
+        for q in range(4):
+            value = value + dot32(everyone[q, rows, :], change[q * block : (q + 1) * block, :])
+        value = value * scale
+        for h in range(2):
+            states_two[h, rows, :] = value[:, h * block : (h + 1) * block]
+            out_copy(t, h).start()
+
+    @pl.loop(0, own // face)
+    def _(t):
+        for h in range(2):
+            out_copy(t, h).wait()
 
 
 def fused(wavefunctions, mass_scale, cell_matrices, connectivity, face_index, domains):
@@ -573,7 +597,8 @@
     scratch = dict(
         matrix=pltpu.VMEM((extent, extent), bf16),
         b=pltpu.VMEM((cells * nodes, share), bf16),
-        picks=pltpu.VMEM((share, nodes), bf16),
+        picks=pltpu.VMEM((nodes, share), bf16),
+        picks_next=pltpu.VMEM((nodes, share), bf16),
         hits=pltpu.VMEM((face, cells * nodes), bf16),
         mass_all=pltpu.VMEM((own, 128), f32),
         face_column=pltpu.VMEM((face, 128), jnp.int32),
@@ -585,7 +610,8 @@
         faces_in=pltpu.VMEM((3, 2, face, block), bf16),
         corner_in=pltpu.VMEM((face, face), bf16),
         rests=pltpu.VMEM((2, extent, 128), bf16),
-        rest_all=pltpu.VMEM((own, 128), f32),
+        rest_all=pltpu.VMEM((extent, 128), f32),
+        lost=pltpu.VMEM((8, share), f32),
         corner_rest=pltpu.VMEM((face, 128), bf16),
         corner_rest_in=pltpu.VMEM((face, 128), bf16),
         added_low=pltpu.VMEM((face, block), bf16),
@@ -601,7 +627,7 @@
         second=pltpu.VMEM((states, width), f32),
         third=pltpu.VMEM((states, width), bf16),
         term=pltpu.VMEM((states, width), bf16),
-        local_sem=dma((6,)),
+        local_sem=dma((2 * own // face,)),
     )
     counts = dict(
         face=(3, 2), corner=(2,), matrix=(extent // face,), rest=(extent // face,), band=(2,),
@@ -611,40 +637,21 @@
     for name, shape in counts.items():
         scratch[name + "_send"] = dma(shape)
         scratch[name + "_recv"] = dma(shape)
-    names = ("conn", "a", "mass", "face", "wave", "everyone_out", "filtered_out", "change", "scale")
-    everyone, filtered, change, scale = pl.pallas_call(
+    names = ("conn_ref", "a_ref", "mass_ref", "face_ref", "wave_ref", "out_ref")
+    return pl.pallas_call(
         functools.partial(fused_kernel, inner, outer, names + tuple(scratch)),
-        out_shape=(
-            jax.ShapeDtypeStruct((4, own, block), bf16),
-            jax.ShapeDtypeStruct((2, own, block), f32),
-            jax.ShapeDtypeStruct((states, width), bf16),
-            jax.ShapeDtypeStruct((8, 128), f32),
-        ),
+        out_shape=jax.ShapeDtypeStruct((own, width), f32),
         in_specs=[vmem] * 5,
-        out_specs=(hbm, hbm, vmem, vmem),
+        out_specs=hbm,
         scratch_shapes=list(scratch.values()),
         compiler_params=pltpu.CompilerParams(
             vmem_limit_bytes=FUSED_LIMIT, collective_id=1, has_side_effects=True
         ),
         name="fused",
     )(connectivity, cell_matrices, mass_scale[None, :], face_index[None, :], wavefunctions)
-    tile = face
-    return pl.pallas_call(
-        rotate_kernel,
-        grid=(own // tile,),
-        out_shape=jax.ShapeDtypeStruct((own, width), f32),
-        in_specs=[
-            pl.BlockSpec((2, tile, block), lambda i: (0, i, 0)),
-            pl.BlockSpec((4, tile, block), lambda i: (0, i, 0)),
-            pl.BlockSpec((states, width), lambda i: (0, 0)),
-            pl.BlockSpec((8, 128), lambda i: (0, 0)),
-        ],
-        out_specs=pl.BlockSpec((tile, width), lambda i: (i, 0)),
-        name="rotate",
-    )(filtered, everyone, change, scale)
-
-
-def fits(own, width, face, domains):
+
+
+def fits(own, width, face, cells, domains):
     return (
         lax.axis_size("band") == 2
         and min(split_domains(domains)) > 1
@@ -653,6 +660,7 @@
         and face % 128 == 0
         and own % face == 0
         and (own + face) % 256 == 0
+        and cells % 2 == 0
     )
 
 
@@ -668,7 +676,7 @@
     face = face_index.shape[0]
     domains = lax.axis_size("dom")
     states = band_width * lax.axis_size("band")
-    if fits(own, band_width, face, domains):
+    if fits(own, band_width, face, connectivity.shape[0], domains):
         return fused(wavefunctions, mass_scale, cell_matrices, connectivity, face_index, domains)
     matrix, rest = domain_operator(cell_matrices, connectivity, own + face)
     face_of = (face_index[:, None] == lax.broadcasted_iota(jnp.int32, (face, own), 1)).astype(bf16)

time: 133 us -> 124 us (0.932)
  Pallas kernels: 132 us -> 119 us
  local copies, waits for them, and re-layouts: 0 us -> 4.64 us
    pallas_call x1 -> x0, Pallas kernels: 9.17 us -> none  [fused(): pl.pallas_call(rotate_kernel, grid=(own // tile,), out_shape=jax.ShapeDty...]
    unnamed x0 -> x1, local copies, waits for them, and re-layouts: none -> 4.64 us
    pallas_call x1, Pallas kernels: 123 us -> 119 us  [fused(): pl.pallas_call(functools.partial(fused_kernel, inner, outer, names + tupl...]
where the time goes in v3:
time: 124 us
  Pallas kernels  119 us (96%)
  local copies, waits for them, and re-layouts  4.64 us (4%)
    pallas_call x1, Pallas kernels, fused(): pl.pallas_call(functools.partial(fused_kernel, inner, outer, names + tupl...  119 us
    unnamed x1, local copies, waits for them, and re-layouts  4.64 us

profile of v3, /device:TPU:0, one launch (start us, length us, event | category | flops | bytes accessed | tf_op | source)
XLA Modules:
  0.0 124.1 jit_solution(224428785398161547)
XLA Ops:
  0.0 119.4 %fused.1 = f32[2048,512]{1,0:T(8,128)} custom-call(s32[8,512]{1,0:T(8,128)} %args_0_.4, bf16[8,512,512]{2,1,0:T(8,128)(2,1)} %args_1_.4, f32[1,2048]{1,0:T(1,128)} %bitcast.2, s32[1,256]{1,0:T(1,128)} %bitcast.3, bf16[2048,512]{1,0:T(8,128)(2,1)} %args_4_.4), custom_call_target="tpu_custom_call" | custom-call | tf_op jit(solution)/shard_map/fused/pallas_call | solution.py:641
  119.5 4.6 %copy.7 = f32[2048,512]{1,0:T(8,128)} copy(f32[2048,512]{1,0:T(8,128)} %fused.1) | data formatting | bytes 8388608

commit v4 on v3

--- a/solution.py
+++ b/solution.py
@@ -152,7 +152,7 @@
 def fused_kernel(inner, outer, names, *args):
     refs = dict(zip(names, args))
     conn_ref, a_ref, mass_ref, face_ref, wave_ref = (refs[n] for n in names[:5])
-    out_ref, change = refs[names[5]], refs["term"]
+    out_ref, scale_ref, change = refs[names[5]], refs[names[6]], refs["term"]
     matrix, b, picks, picks_next, hits = (
         refs[n] for n in ("matrix", "b", "picks", "picks_next", "hits")
     )
@@ -532,7 +532,7 @@
             trace = trace + jnp.sum(gathered[q, c].astype(f32) * unit)
     mean_eigen = jnp.full((1, 1), trace, f32) / states
     inverse = 1.0 / mean_eigen
-    scale = lax.rsqrt(mean_eigen)
+    scale_ref[...] = jnp.broadcast_to(lax.rsqrt(mean_eigen), scale_ref.shape)
     for q in range(2):
         for c, (i, j) in enumerate(upper_blocks(q)):
             value = gathered[q, c].astype(f32) * inverse
@@ -570,7 +570,6 @@
         value = jnp.concatenate([states_one[0, rows, :], states_one[1, rows, :]], axis=1)
         for q in range(4):
             value = value + dot32(everyone[q, rows, :], change[q * block : (q + 1) * block, :])
-        value = value * scale
         for h in range(2):
             states_two[h, rows, :] = value[:, h * block : (h + 1) * block]
             out_copy(t, h).start()
@@ -637,18 +636,22 @@
     for name, shape in counts.items():
         scratch[name + "_send"] = dma(shape)
         scratch[name + "_recv"] = dma(shape)
-    names = ("conn_ref", "a_ref", "mass_ref", "face_ref", "wave_ref", "out_ref")
-    return pl.pallas_call(
+    names = ("conn_ref", "a_ref", "mass_ref", "face_ref", "wave_ref", "out_ref", "scale_ref")
+    turned, scale = pl.pallas_call(
         functools.partial(fused_kernel, inner, outer, names + tuple(scratch)),
-        out_shape=jax.ShapeDtypeStruct((own, width), f32),
+        out_shape=(
+            jax.ShapeDtypeStruct((own, width), f32),
+            jax.ShapeDtypeStruct((1, width), f32),
+        ),
         in_specs=[vmem] * 5,
-        out_specs=hbm,
+        out_specs=(hbm, vmem),
         scratch_shapes=list(scratch.values()),
         compiler_params=pltpu.CompilerParams(
             vmem_limit_bytes=FUSED_LIMIT, collective_id=1, has_side_effects=True
         ),
         name="fused",
     )(connectivity, cell_matrices, mass_scale[None, :], face_index[None, :], wavefunctions)
+    return turned * scale
 
 
 def fits(own, width, face, cells, domains):

time: 124 us -> 125 us (level)
  other arithmetic: 0 us -> 4.72 us
  local copies, waits for them, and re-layouts: 4.64 us -> 0 us
    mul x0 -> x1, other arithmetic: none -> 4.72 us  [fused(): return turned * scale]
    unnamed x1 -> x0, local copies, waits for them, and re-layouts: 4.64 us -> none
where the time goes in v4:
time: 125 us
  Pallas kernels  120 us (96%)
  other arithmetic  4.72 us (4%)
    pallas_call x1, Pallas kernels, fused(): pl.pallas_call(functools.partial(fused_kernel, inner, outer, names + tupl...  120 us
    mul x1, other arithmetic, fused(): return turned * scale  4.72 us

profile of v4, /device:TPU:0, one launch (start us, length us, event | category | flops | bytes accessed | tf_op | source)
XLA Modules:
  0.0 124.8 jit_solution(14114289418533304475)
XLA Ops:
  0.0 120.1 %fused.1 = (f32[2048,512]{1,0:T(8,128)}, f32[1,512]{1,0:T(1,128)}) custom-call(s32[8,512]{1,0:T(8,128)} %args_0_.4, bf16[8,512,512]{2,1,0:T(8,128)(2,1)} %args_1_.4, f32[1,2048]{1,0:T(1,128)} %bitcast.3, s32[1,256]{1,0:T(1,128)} %bitcast.5, bf16[2048,512]{1,0:T(8,128)(2,1)} %args_4_.4), custom_call_target="tpu_custom_call" | custom-call | tf_op jit(solution)/shard_map/fused/pallas_call | solution.py:640
  120.1 4.7 %broadcast_multiply_fusion = f32[2048,512]{1,0:T(8,128)} fusion(f32[2048,512]{1,0:T(8,128)} %get-tuple-element.7, f32[512]{0:T(512)} %bitcast.4), kind=kLoop, calls=%fused_computation | loop fusion | flops 1048576 | bytes 8390656 | tf_op jit(solution)/shard_map/mul | solution.py:654
